TPU v7x, 32 devices: a whole 2x2x4 slice. The times are simulated.
32 devices in a mesh: section: 2 (over core), dp: 4 (over y, x), tensor: 4 (over z).
Axes of the slice: x: 2, y: 2, z: 4, core: 2. Of those that a mesh axis runs over, the one named last changes fastest.
Arguments:
- boundary: float32 [2, 12, 256, 2048], P('section', 'dp', 'tensor'), may hold values from -24 to 24
- segments: int32 [12, 256], P('dp'), may hold values from 0 to 3, never falling along the last dimension, each value on 1 to 128 neighbouring positions
- w_qkv: bfloat16 [2, 2048, 3, 2048], P('section', 'dp', None, 'tensor'), may hold values from -0.125 to 0.125
- w_out: bfloat16 [2, 2048, 2048], P('section', 'tensor', 'dp'), may hold values from -0.125 to 0.125
- w_gate_up: bfloat16 [2, 2048, 2, 8192], P('section', 'dp', None, 'tensor'), may hold values from -0.125 to 0.125
- w_down: bfloat16 [2, 8192, 2048], P('section', 'tensor', 'dp'), may hold values from -0.0625 to 0.0625
- gains: bfloat16 [2, 4, 2048], P('section', None, 'dp'), may hold values from 0.5 to 2
Outputs:
- section_out: float32 [2, 12, 256, 2048], P('section', 'dp', 'tensor')
- section_grad: float32 [2, 12, 256, 2048], P('section', 'dp', 'tensor')
- grad_qkv: float32 [2, 2048, 3, 2048], P('section', 'dp', None, 'tensor')
- grad_attn_out: float32 [2, 2048, 2048], P('section', 'tensor', 'dp')
- grad_gate_up: float32 [2, 2048, 2, 8192], P('section', 'dp', None, 'tensor')
- grad_down: float32 [2, 8192, 2048], P('section', 'tensor', 'dp')
- grad_gains: float32 [2, 4, 2048], P('section', None, 'dp')
Inputs may be any that keep to these rules, and one draw needn't show every extreme that they name: `segments`: segment ids never fall along a sequence; each of the 4 documents of a sequence covers 1 to 128 positions.
All inputs are finite; a program needn't handle non-finite values.
Results may differ from a plain program's by a relative error of at most 0.035.
Values may be sent and summed in bfloat16 or wider, within the bound.
No kernel may reach another device: no remote copies, remote signals or barrier semaphores. Data moves between devices by JAX's collectives and lax.ppermute only.
A program may use at most 384 MiB of HBM per device.

v0:
```python
import jax
import jax.numpy as jnp
from jax import lax
from jax.sharding import PartitionSpec as P


D = 2048
HD = 128


EPS = 1e-06
THETA = 500000.0


def matmul(left, right):
    return jnp.dot(left, right, preferred_element_type=jnp.float32)


def inner_left(left, right):
    return lax.dot_general(
        left, right, (((0,), (0,)), ((), ())), preferred_element_type=jnp.float32
    )


def inner_right(left, right):
    return lax.dot_general(
        left, right, (((1,), (1,)), ((), ())), preferred_element_type=jnp.float32
    )


def rms_scale(vectors):
    return lax.rsqrt(jnp.mean(vectors * vectors, axis=-1, keepdims=True) + EPS)


def swap_cores(block):
    return lax.ppermute(block, "section", [(0, 1), (1, 0)])


def one_way(block, source):
    return lax.ppermute(block, "section", [(source, 1 - source)])


def from_ahead(block, distance):
    size = lax.axis_size("tensor")
    return lax.ppermute(block, "tensor", [(i, (i - distance) % size) for i in range(size)])


def to_ahead(block, distance):
    size = lax.axis_size("tensor")
    return lax.ppermute(block, "tensor", [(i, (i + distance) % size) for i in range(size)])


def square():
    return lax.axis_size("dp") == 4


def across(block, flip):
    return lax.ppermute(block, "dp", [(i, i ^ flip) for i in range(4)])


def local_blocks(array):
    if not square():
        return array
    rank = lax.axis_index("dp")
    width = array.shape[-1] // 4
    return jnp.concatenate(
        [
            lax.dynamic_slice_in_dim(array, (rank ^ j) * width, width, array.ndim - 1)
            for j in range(4)
        ],
        axis=-1,
    )


def gather_blocks(block):
    if not square():
        return list(lax.all_gather(block, "dp", axis=0, tiled=False))
    half = block.shape[0] // 2
    by_x = across(block, 1)
    by_y = across(block, 2)
    low = across(by_y[:half], 1)
    high = across(by_x[half:], 2)
    return [block, by_x, by_y, jnp.concatenate([low, high], axis=0)]


def scatter_blocks(blocks):
    wire = jnp.bfloat16
    if not square():
        whole = jnp.concatenate([block.astype(wire) for block in blocks], axis=0)
        return lax.psum_scatter(whole, "dp", scatter_dimension=0, tiled=True).astype(jnp.float32)
    half = blocks[0].shape[0] // 2
    own, to_x, to_y, to_far = [block.astype(wire) for block in blocks]
    by_x = across(jnp.concatenate([to_far[:half], to_x[:half]], axis=0), 1)
    by_y = across(jnp.concatenate([to_far[half:], to_y[half:]], axis=0), 2)

    def added(left, right):
        return left.astype(jnp.float32) + right.astype(jnp.float32)

    high = across(added(to_x[half:], by_y[:half]).astype(wire), 1)
    low = across(added(to_y[:half], by_x[:half]).astype(wire), 2)
    by_x, by_y, low, high = lax.optimization_barrier((by_x, by_y, low, high))
    low = added(own[:half], by_x[half:]) + low.astype(jnp.float32)
    high = added(own[half:], by_y[half:]) + high.astype(jnp.float32)
    return jnp.concatenate([low, high], axis=0)


def split_last(array):
    return jnp.split(array, lax.axis_size("dp"), axis=-1)


def split_first(array):
    return jnp.split(array, lax.axis_size("dp"), axis=0)


def gather_tokens(rows):
    size = lax.axis_size("tensor")
    slots = [rows]
    for j in range(1, size):
        slots.append(from_ahead(rows, j))
    mine = jnp.stack(slots, axis=1)
    other = swap_cores(mine)
    return jnp.concatenate([mine, other], axis=1)


def scatter_tokens(partial):
    size = lax.axis_size("tensor")
    other = swap_cores(partial[:, size:].astype(jnp.bfloat16))
    chip = partial[:, :size] + other.astype(jnp.float32)
    total = chip[:, 0]
    sent = chip.astype(jnp.bfloat16)
    for j in range(1, size):
        total = total + to_ahead(sent[:, j], j).astype(jnp.float32)
    return total


def sum_heads(parts, seqs):
    size = lax.axis_size("tensor")
    split = parts.reshape(parts.shape[0], seqs, 2, size, -1)
    other = swap_cores(split)
    chip = split + other[:, :, ::-1]
    total = chip
    for j in range(1, size):
        ahead = from_ahead(chip, j)
        total = total + jnp.roll(ahead, j, axis=3)
    return total.reshape(parts.shape)


def sum_gains(part):
    chip = part + swap_cores(part)
    total = chip
    for j in range(1, lax.axis_size("tensor")):
        total = total + from_ahead(chip, j)
    return total


def local_order(table, section_index, tensor_rank):
    seqs, length = table.shape
    size = lax.axis_size("tensor")
    split = table.reshape(seqs, size, 2, length // (2 * size))
    twice = jnp.concatenate([split, split], axis=1)
    turned = lax.dynamic_slice_in_dim(twice, tensor_rank, size, 1)
    turned = jnp.where(section_index == 0, turned, turned[:, :, ::-1])
    return jnp.transpose(turned, (0, 2, 1, 3)).reshape(seqs, length)


def doc_tables(seg_rows, section_index, tensor_rank):
    same_doc = seg_rows[:, :, None] == seg_rows[:, None, :]
    index_row = jnp.arange(seg_rows.shape[1], dtype=jnp.int32)
    earlier = index_row[None, :] < index_row[:, None]
    positions = jnp.sum((same_doc & earlier[None]).astype(jnp.int32), axis=-1)
    positions = local_order(positions, section_index, tensor_rank)
    segs = local_order(seg_rows, section_index, tensor_rank)
    order = local_order(
        jnp.broadcast_to(index_row[None], seg_rows.shape), section_index, tensor_rank
    )
    visible = (segs[:, :, None] == segs[:, None, :]) & (order[:, None, :] <= order[:, :, None])
    half_dim = HD // 2
    inverse_freq = THETA ** (-(jnp.arange(half_dim, dtype=jnp.float32) * (2.0 / HD)))
    angles = positions.astype(jnp.float32)[..., None] * inverse_freq
    return (visible, jnp.cos(angles), jnp.sin(angles))


def rotate(vectors, cosine, sine_part):
    half_dim = HD // 2
    front_half = vectors[..., :half_dim]
    back_half = vectors[..., half_dim:]
    cos_wide = cosine[:, :, None, :]
    sin_wide = sine_part[:, :, None, :]
    return jnp.concatenate(
        [
            front_half * cos_wide - back_half * sin_wide,
            back_half * cos_wide + front_half * sin_wide,
        ],
        axis=-1,
    )


def masked_scores(query_rot, key_rot, visible):
    scores = jnp.einsum(
        "bshe,bthe->bhst", query_rot, key_rot, preferred_element_type=jnp.float32
    ) * HD ** (-0.5)
    return jnp.where(visible[:, None], scores, -jnp.inf)


def log_norm(masked):
    row_max = jnp.max(masked, axis=-1, keepdims=True)
    return row_max + jnp.log(jnp.sum(jnp.exp(masked - row_max), axis=-1, keepdims=True))


class Layer:
    def __init__(self, w_qkv, w_out, w_gate_up, w_down, gains, head_slot):
        self.w_qkv = w_qkv
        self.w_out = w_out
        self.w_gate_up = w_gate_up
        self.w_down = w_down
        self.gains = gains
        width = w_out.shape[0]
        whole = local_blocks(gains)
        self.query_gain = lax.dynamic_slice_in_dim(whole[0], head_slot * width, width)
        self.key_gain = lax.dynamic_slice_in_dim(whole[1], head_slot * width, width)
        self.head_slot = head_slot

    def attend(self, layer_in, tables):
        visible, cosine, sine_part = tables
        full = gather_tokens(layer_in.astype(jnp.bfloat16))
        seqs, slots, rows, _ = full.shape
        length = slots * rows
        tokens = seqs * length
        full = full.reshape(tokens, D)
        width = self.w_out.shape[0]
        heads = width // HD
        qkv = matmul(full, self.w_qkv)
        queries = qkv[:, :width]
        key_vecs = qkv[:, width : 2 * width]
        values = qkv[:, 2 * width :].astype(jnp.bfloat16).reshape(seqs, length, heads, HD)
        squares = sum_heads(
            jnp.stack([jnp.sum(queries * queries, axis=-1), jnp.sum(key_vecs * key_vecs, axis=-1)]),
            seqs,
        )
        scales = lax.rsqrt(squares / D + EPS)
        query_scale = scales[0][:, None]
        key_scale = scales[1][:, None]
        query_hat = queries * query_scale
        key_hat = key_vecs * key_scale
        query_rot = rotate(
            (query_hat * self.query_gain).reshape(seqs, length, heads, HD), cosine, sine_part
        ).astype(jnp.bfloat16)
        key_rot = rotate(
            (key_hat * self.key_gain).reshape(seqs, length, heads, HD), cosine, sine_part
        ).astype(jnp.bfloat16)
        masked = masked_scores(query_rot, key_rot, visible)
        log_total = log_norm(masked)
        probs = jnp.exp(masked - log_total)
        mix = jnp.einsum(
            "bhst,bthe->bshe",
            probs.astype(jnp.bfloat16),
            values,
            preferred_element_type=jnp.float32,
        )
        mix = mix.astype(jnp.bfloat16).reshape(tokens, width)
        attn = scatter_tokens(matmul(mix, self.w_out).reshape(seqs, slots, rows, D))
        attn_scale = rms_scale(attn)
        attn_hat = attn * attn_scale
        hidden = layer_in + attn_hat * self.gains[2]
        kept = dict(
            full=full,
            query_hat=query_hat,
            key_hat=key_hat,
            query_scale=query_scale,
            key_scale=key_scale,
            query_rot=query_rot,
            key_rot=key_rot,
            values=values,
            log_total=log_total,
            mix=mix,
            attn_hat=attn_hat,
            attn_scale=attn_scale,
            tables=tables,
        )
        return hidden, kept

    def feed(self, hidden, kept):
        full = gather_tokens(hidden.astype(jnp.bfloat16))
        seqs, slots, rows, _ = full.shape
        full = full.reshape(seqs * slots * rows, D)
        units = self.w_down.shape[0]
        gate_up = matmul(full, self.w_gate_up)
        gate = gate_up[:, :units]
        up = gate_up[:, units:]
        swiglu = (jax.nn.silu(gate) * up).astype(jnp.bfloat16)
        ffn = scatter_tokens(matmul(swiglu, self.w_down).reshape(seqs, slots, rows, D))
        ffn_scale = rms_scale(ffn)
        ffn_hat = ffn * ffn_scale
        output = hidden + ffn_hat * self.gains[3]
        kept = dict(
            kept,
            full_hidden=full,
            gate=gate,
            up=up,
            swiglu=swiglu,
            ffn_hat=ffn_hat,
            ffn_scale=ffn_scale,
        )
        return output, kept

    def feed_back(self, back_output, kept):
        ffn_hat = kept["ffn_hat"]
        gain_ffn = jnp.sum(back_output * ffn_hat, axis=(0, 1))
        back_hat = back_output * self.gains[3]
        back_ffn = kept["ffn_scale"] * (
            back_hat - ffn_hat * jnp.mean(back_hat * ffn_hat, axis=-1, keepdims=True)
        )
        back_ffn, gain_ffn = lax.optimization_barrier((back_ffn.astype(jnp.bfloat16), gain_ffn))
        full = gather_tokens(back_ffn)
        shape = full.shape
        full = full.reshape(-1, D)
        grad_down = inner_left(kept["swiglu"], full)
        back_swiglu = inner_right(full, self.w_down)
        gate = kept["gate"]
        up = kept["up"]
        sigmoid_gate = jax.nn.sigmoid(gate)
        back_gate = back_swiglu * up * sigmoid_gate * (1.0 + gate * (1.0 - sigmoid_gate))
        back_up = back_swiglu * jax.nn.silu(gate)
        back_gate_up = jnp.concatenate([back_gate, back_up], axis=1).astype(jnp.bfloat16)
        back_hidden = back_output + scatter_tokens(
            inner_right(back_gate_up, self.w_gate_up).reshape(shape)
        )
        grad_gate_up = inner_left(kept["full_hidden"], back_gate_up)
        return back_hidden, dict(down=grad_down, gate_up=grad_gate_up, gain_ffn=gain_ffn)

    def attend_back(self, back_hidden, kept):
        visible, cosine, sine_part = kept["tables"]
        attn_hat = kept["attn_hat"]
        gain_attn = jnp.sum(back_hidden * attn_hat, axis=(0, 1))
        back_hat = back_hidden * self.gains[2]
        back_attn = kept["attn_scale"] * (
            back_hat - attn_hat * jnp.mean(back_hat * attn_hat, axis=-1, keepdims=True)
        )
        back_attn, gain_attn = lax.optimization_barrier(
            (back_attn.astype(jnp.bfloat16), gain_attn)
        )
        full = gather_tokens(back_attn)
        shape = full.shape
        full = full.reshape(-1, D)
        tokens = full.shape[0]
        query_rot = kept["query_rot"]
        key_rot = kept["key_rot"]
        values = kept["values"]
        heads_shape = values.shape
        grad_out = inner_left(kept["mix"], full)
        back_mix = inner_right(full, self.w_out).astype(jnp.bfloat16).reshape(heads_shape)
        masked = masked_scores(query_rot, key_rot, visible)
        probs = jnp.exp(masked - kept["log_total"])
        back_values = jnp.einsum(
            "bhst,bshe->bthe",
            probs.astype(jnp.bfloat16),
            back_mix,
            preferred_element_type=jnp.float32,
        ).astype(jnp.bfloat16)
        back_probs = jnp.einsum(
            "bshe,bthe->bhst", back_mix, values, preferred_element_type=jnp.float32
        )
        row_dot = jnp.sum(probs * back_probs, axis=-1, keepdims=True)
        back_scores = (probs * (back_probs - row_dot) * HD ** (-0.5)).astype(jnp.bfloat16)
        back_query_rot = jnp.einsum(
            "bhst,bthe->bshe", back_scores, key_rot, preferred_element_type=jnp.float32
        )
        back_key_rot = jnp.einsum(
            "bhst,bshe->bthe", back_scores, query_rot, preferred_element_type=jnp.float32
        )
        width = self.w_out.shape[0]
        back_query_gained = rotate(back_query_rot, cosine, -sine_part).reshape(tokens, width)
        back_key_gained = rotate(back_key_rot, cosine, -sine_part).reshape(tokens, width)
        query_hat = kept["query_hat"]
        key_hat = kept["key_hat"]
        gain_query = jnp.sum(back_query_gained * query_hat, axis=0)
        gain_key = jnp.sum(back_key_gained * key_hat, axis=0)
        back_query_hat = back_query_gained * self.query_gain
        back_key_hat = back_key_gained * self.key_gain
        dots = sum_heads(
            jnp.stack(
                [
                    jnp.sum(back_query_hat * query_hat, axis=-1),
                    jnp.sum(back_key_hat * key_hat, axis=-1),
                ]
            ),
            shape[0],
        )
        back_query = kept["query_scale"] * (back_query_hat - query_hat * (dots[0] / D)[:, None])
        back_key = kept["key_scale"] * (back_key_hat - key_hat * (dots[1] / D)[:, None])
        back_qkv = jnp.concatenate(
            [
                back_query.astype(jnp.bfloat16),
                back_key.astype(jnp.bfloat16),
                back_values.reshape(tokens, width),
            ],
            axis=1,
        )
        back_input = back_hidden + scatter_tokens(inner_right(back_qkv, self.w_qkv).reshape(shape))
        grad_qkv = inner_left(kept["full"], back_qkv)
        zero_width = jnp.zeros((2, D), jnp.float32)
        start = self.head_slot * width
        gain_heads = local_blocks(
            lax.dynamic_update_slice(zero_width, jnp.stack([gain_query, gain_key]), (0, start))
        )
        gain_part = jnp.concatenate([gain_heads, gain_attn[None]], axis=0)
        return back_input, dict(out=grad_out, qkv=grad_qkv, gains=gain_part)


def whole_step(boundary, segments, w_qkv, w_out, w_gate_up, w_down, gains):
    section_index = lax.axis_index("section")
    tensor_rank = lax.axis_index("tensor")
    first = section_index == 0

    def shared(block, axis):
        half = block.shape[axis] // 2
        kept = lax.dynamic_slice_in_dim(block, section_index * half, half, axis)
        sent = lax.dynamic_slice_in_dim(block, (1 - section_index) * half, half, axis)
        received = swap_cores(sent)
        return jnp.where(first, kept, received), jnp.where(first, received, kept)

    rows_in, rows_back = [local_blocks(rows) for rows in shared(boundary[0], 1)]
    model = w_qkv.shape[1]
    qkv_halves = [half.reshape(model, -1) for half in shared(w_qkv[0], 2)]
    out_halves = shared(w_out[0], 0)
    gate_up_halves = [half.reshape(model, -1) for half in shared(w_gate_up[0], 2)]
    down_halves = shared(w_down[0], 0)
    other_gains = swap_cores(gains[0])
    both_gains = jnp.concatenate(
        [jnp.where(first, gains[0], other_gains), jnp.where(first, other_gains, gains[0])], axis=0
    )
    all_gains = jnp.concatenate(gather_blocks(both_gains), axis=1)
    head_slot = tensor_rank * 2 + section_index
    layers = []
    for index in range(2):
        layers.append(
            Layer(
                jnp.concatenate(gather_blocks(qkv_halves[index]), axis=0),
                jnp.concatenate(gather_blocks(out_halves[index]), axis=1),
                jnp.concatenate(gather_blocks(gate_up_halves[index]), axis=0),
                jnp.concatenate(gather_blocks(down_halves[index]), axis=1),
                all_gains[4 * index : 4 * index + 4],
                head_slot,
            )
        )
    tables = doc_tables(segments, section_index, tensor_rank)
    state = rows_in
    kept = []
    outs = []
    for layer in layers:
        hidden, now = layer.attend(state, tables)
        state, now = layer.feed(hidden, now)
        kept.append(now)
        outs.append(state)
    state = rows_back
    backs = [None, None]
    all_grads = [None, None]
    width = w_out.shape[1] // 2
    for index in (1, 0):
        hidden, feed_grads = layers[index].feed_back(state, kept[index])
        down = scatter_blocks(split_last(feed_grads["down"]))
        gate_up = scatter_blocks(split_first(feed_grads["gate_up"]))
        state, grads = layers[index].attend_back(hidden, kept[index])
        backs[index] = state
        qkv = scatter_blocks(split_first(grads["qkv"]))
        gain_part = jnp.concatenate([grads["gains"], feed_grads["gain_ffn"][None]], axis=0)
        if index == 1:
            state, gain_part = lax.optimization_barrier((state, gain_part))
        gain_rows = sum_gains(gain_part)
        out = scatter_blocks(
            split_last(
                jnp.concatenate([grads["out"], jnp.pad(gain_rows, ((0, 28), (0, 0)))], axis=0)
            ),
        )
        all_grads[index] = dict(
            down=down.astype(jnp.bfloat16),
            gate_up=gate_up.astype(jnp.bfloat16),
            qkv=qkv.astype(jnp.bfloat16),
            out=out[:width].astype(jnp.bfloat16),
            gains=out[width : width + 4],
        )
    first_grads, second_grads = all_grads

    def collected(name, axis, shape):
        mine_first = first_grads[name].reshape(shape)
        mine_second = second_grads[name].reshape(shape)
        to_second = one_way(mine_second, 0)
        to_first = one_way(mine_first, 1)
        low = jnp.where(first, mine_first, to_second)
        high = jnp.where(first, to_first, mine_second)
        return jnp.concatenate([low, high], axis=axis).astype(jnp.float32)[None]

    def placed(first_rows, second_rows):
        to_second = one_way(second_rows, 0)
        to_first = one_way(first_rows, 1)
        low = jnp.where(first, first_rows, to_second)
        high = jnp.where(first, to_first, second_rows)
        return local_blocks(jnp.concatenate([low, high], axis=1))[None]

    units = w_down.shape[1] // 2
    return (
        placed(outs[0], outs[1]),
        placed(backs[0], backs[1]),
        collected("qkv", 2, (model, 3, width)),
        collected("out", 0, (width, w_out.shape[2])),
        collected("gate_up", 2, (model, 2, units)),
        collected("down", 0, (units, w_down.shape[2])),
        jnp.where(first, first_grads["gains"], second_grads["gains"])[None],
    )


def solution(mesh):
    return jax.shard_map(
        whole_step,
        mesh=mesh,
        in_specs=(
            P("section", "dp", "tensor", None),
            P("dp", None),
            P("section", "dp", None, "tensor"),
            P("section", "tensor", "dp"),
            P("section", "dp", None, "tensor"),
            P("section", "tensor", "dp"),
            P("section", None, "dp"),
        ),
        out_specs=(
            P("section", "dp", "tensor", None),
            P("section", "dp", "tensor", None),
            P("section", "dp", None, "tensor"),
            P("section", "tensor", "dp"),
            P("section", "dp", None, "tensor"),
            P("section", "tensor", "dp"),
            P("section", None, "dp"),
        ),
        check_vma=False,
    )
```

profile of v0, /device:TPU:0, one launch (start us, length us, event | category | flops | bytes accessed | tf_op | source)
XLA Modules:
  0.0 1392.2 jit_solution(3009040998479831008)
XLA Ops:
  43.7 23.7 %collective-permute-done.2 = bf16[3,32,2048]{2,1,0:T(8,128)(2,1)S(1)} collective-permute-done((bf16[3,32,2048]{2,1,0:T(8,128)(2,1)S(1)}, bf16[3,32,2048]{2,1,0:T(8,128)(2,1)S(1)}, u32[]{:S(2)}, u32[]{:S(2)}) %collective-permute-start.2) | collective-permute-done | bytes 393248 | tf_op jit(solution)/shard_map/ppermute | solution.py:45
  68.3 18.2 %collective-permute-done.7 = bf16[512,768]{0,1:T(8,128)(2,1)S(1)} collective-permute-done((bf16[512,768]{0,1:T(8,128)(2,1)S(1)}, bf16[512,768]{0,1:T(8,128)(2,1)S(1)}, u32[]{:S(2)}, u32[]{:S(2)}) %collective-permute-start.7) | collective-permute-done | bytes 786464 | tf_op jit(solution)/shard_map/ppermute | solution.py:58
  165.4 13.0 collective-permute-done.39
  184.4 12.7 collective-permute-done.26
  207.1 17.6 %collective-permute-done.33 = bf16[512,2048]{1,0:T(8,128)(2,1)S(1)} collective-permute-done((bf16[512,2048]{1,0:T(8,128)(2,1)S(1)}, bf16[512,2048]{1,0:T(8,128)(2,1)S(1)}, u32[]{:S(2)}, u32[]{:S(2)}) %collective-permute-start.33) | collective-permute-done | bytes 2097184 | tf_op jit(solution)/shard_map/ppermute | solution.py:58
  227.6 12.7 collective-permute-done.29
  242.9 13.8 collective-permute-done.35
  299.5 15.9 %collective-permute-done.44 = bf16[3,32,2048]{2,1,0:T(8,128)(2,1)S(1)} collective-permute-done((bf16[3,32,2048]{2,1,0:T(8,128)(2,1)S(1)}, bf16[3,32,2048]{2,1,0:T(8,128)(2,1)S(1)}, u32[]{:S(2)}, u32[]{:S(2)}) %collective-permute-start.44) | collective-permute-done | bytes 393248 | tf_op jit(solution)/shard_map/ppermute | solution.py:50
  333.8 26.5 %collective-permute-done.47 = bf16[3,32,2048]{2,1,0:T(8,128)(2,1)S(1)} collective-permute-done((bf16[3,32,2048]{2,1,0:T(8,128)(2,1)S(1)}, bf16[3,32,2048]{2,1,0:T(8,128)(2,1)S(1)}, u32[]{:S(2)}, u32[]{:S(2)}) %collective-permute-start.47) | collective-permute-done | bytes 393248 | tf_op jit(solution)/shard_map/ppermute | solution.py:45
  417.5 64.3 %collective-permute-done.75 = bf16[1024,512]{1,0:T(8,128)(2,1)S(1)} collective-permute-done((bf16[1024,512]{1,0:T(8,128)(2,1)S(1)}, bf16[1024,512]{1,0:T(8,128)(2,1)S(1)}, u32[]{:S(2)}, u32[]{:S(2)}) %collective-permute-start.75) | collective-permute-done | bytes 1048608 | tf_op jit(solution)/shard_map/ppermute | solution.py:58
  490.3 11.5 collective-permute-done.64
  522.5 22.3 %collective-permute-done.67 = bf16[3,32,2048]{2,1,0:T(8,128)(2,1)S(1)} collective-permute-done((bf16[3,32,2048]{2,1,0:T(8,128)(2,1)S(1)}, bf16[3,32,2048]{2,1,0:T(8,128)(2,1)S(1)}, u32[]{:S(2)}, u32[]{:S(2)}) %collective-permute-start.67) | collective-permute-done | bytes 393248 | tf_op jit(solution)/shard_map/ppermute | solution.py:45
  548.9 10.3 fusion.213
  583.4 16.3 %collective-permute-done.80 = bf16[3,32,2048]{2,1,0:T(8,128)(2,1)S(1)} collective-permute-done((bf16[3,32,2048]{2,1,0:T(8,128)(2,1)S(1)}, bf16[3,32,2048]{2,1,0:T(8,128)(2,1)S(1)}, u32[]{:S(2)}, u32[]{:S(2)}) %collective-permute-start.80) | collective-permute-done | bytes 393248 | tf_op jit(solution)/shard_map/ppermute | solution.py:50
  601.1 10.3 collective-permute-start.84
  621.0 24.4 %collective-permute-done.85 = bf16[3,32,2048]{2,1,0:T(8,128)(2,1)S(1)} collective-permute-done((bf16[3,32,2048]{2,1,0:T(8,128)(2,1)S(1)}, bf16[3,32,2048]{2,1,0:T(8,128)(2,1)S(1)}, u32[]{:S(2)}, u32[]{:S(2)}) %collective-permute-start.85) | collective-permute-done | bytes 393248 | tf_op jit(solution)/shard_map/ppermute | solution.py:45
  655.1 17.3 %multiply_convert_fusion.3 = (bf16[768,1024]{1,0:T(8,128)(2,1)S(1)}, bf16[768,1024]{1,0:T(8,128)(2,1)}) fusion(f32[768,2048]{1,0:T(8,128)S(1)} %fusion.213, bf16[768,2048]{1,0:T(8,128)(2,1)} %bitcast.480, bf16[512,512]{1,0:T(8,128)(2,1)S(1)} %copy-done.202, bf16[512,512]{1,0:T(8,128)(2,1)S(1)} %collective-permute-done.76, ...), kind=kOutput, calls=%fused_computation.36 | convolution fusion | flops 3252420608 | bytes 16777216 | tf_op jit(solution)/shard_map/dot_general | solution.py:26
  672.5 10.4 fusion.9
  697.6 13.8 collective-permute-done.169
  735.8 15.7 %collective-permute-done.90 = bf16[3,32,2048]{2,1,0:T(8,128)(2,1)S(1)} collective-permute-done((bf16[3,32,2048]{2,1,0:T(8,128)(2,1)S(1)}, bf16[3,32,2048]{2,1,0:T(8,128)(2,1)S(1)}, u32[]{:S(2)}, u32[]{:S(2)}) %collective-permute-start.90) | collective-permute-done | bytes 393248 | tf_op jit(solution)/shard_map/ppermute | solution.py:50
  777.6 20.4 %collective-permute-done.93 = bf16[3,32,2048]{2,1,0:T(8,128)(2,1)S(1)} collective-permute-done((bf16[3,32,2048]{2,1,0:T(8,128)(2,1)S(1)}, bf16[3,32,2048]{2,1,0:T(8,128)(2,1)S(1)}, u32[]{:S(2)}, u32[]{:S(2)}) %collective-permute-start.93) | collective-permute-done | bytes 393248 | tf_op jit(solution)/shard_map/ppermute | solution.py:45
  925.5 13.0 collective-permute-done.102
  966.6 14.1 %collective-permute-done.105 = bf16[3,32,2048]{2,1,0:T(8,128)(2,1)S(1)} collective-permute-done((bf16[3,32,2048]{2,1,0:T(8,128)(2,1)S(1)}, bf16[3,32,2048]{2,1,0:T(8,128)(2,1)S(1)}, u32[]{:S(2)}, u32[]{:S(2)}) %collective-permute-start.105) | collective-permute-done | bytes 393248 | tf_op jit(solution)/shard_map/ppermute | solution.py:45
  992.7 15.0 %multiply_convert_fusion.1 = (bf16[768,1024]{1,0:T(8,128)(2,1)}, bf16[768,1024]{1,0:T(8,128)(2,1)}) fusion(f32[768,2048]{1,0:T(8,128)S(1)} %bitcast.442, bf16[768,2048]{1,0:T(8,128)(2,1)S(1)} %bitcast.482, bf16[512,512]{1,0:T(8,128)(2,1)S(1)} %copy-done.200, bf16[512,512]{1,0:T(8,128)(2,1)S(1)} %copy-done.198, bf16[1024,512]{1,0:T(8,128)(2,1)S(1)} %copy-done.146, ...), kind=kOutput, calls=%fused_computation.34 | convolution fusion | flops 3252420608 | bytes 16777216 | tf_op jit(solution)/shard_map/dot_general | solution.py:26
  1007.8 10.2 fusion.8
  1032.9 21.4 %collective-permute-done.165 = bf16[1024,512]{1,0:T(8,128)(2,1)} collective-permute-done((bf16[1024,512]{1,0:T(8,128)(2,1)S(1)}, bf16[1024,512]{1,0:T(8,128)(2,1)}, u32[]{:S(2)}, u32[]{:S(2)}) %collective-permute-start.165) | collective-permute-done | bytes 1048608 | tf_op jit(solution)/shard_map/ppermute | solution.py:58
  1060.2 49.7 %collective-permute-done.166 = bf16[512,512]{1,0:T(8,128)(2,1)S(1)} collective-permute-done((bf16[512,512]{1,0:T(8,128)(2,1)S(1)}, bf16[512,512]{1,0:T(8,128)(2,1)S(1)}, u32[]{:S(2)}, u32[]{:S(2)}) %collective-permute-start.166) | collective-permute-done | bytes 524320 | tf_op jit(solution)/shard_map/ppermute | solution.py:58
  1127.4 12.0 collective-permute-done.110
  1144.6 12.5 collective-permute-start.112
  1166.5 24.3 %collective-permute-done.113 = bf16[3,32,2048]{2,1,0:T(8,128)(2,1)S(1)} collective-permute-done((bf16[3,32,2048]{2,1,0:T(8,128)(2,1)S(1)}, bf16[3,32,2048]{2,1,0:T(8,128)(2,1)S(1)}, u32[]{:S(2)}, u32[]{:S(2)}) %collective-permute-start.113) | collective-permute-done | bytes 393248 | tf_op jit(solution)/shard_map/ppermute | solution.py:45
  1199.3 16.8 %collective-permute-done.156 = bf16[256,2048]{0,1:T(8,128)(2,1)S(1)} collective-permute-done((bf16[256,2048]{0,1:T(8,128)(2,1)S(1)}, bf16[256,2048]{0,1:T(8,128)(2,1)S(1)}, u32[]{:S(2)}, u32[]{:S(2)}) %collective-permute-start.156) | collective-permute-done | bytes 1048608 | tf_op jit(solution)/shard_map/ppermute | solution.py:58
  1351.3 17.7 %collective-permute-done.122 = bf16[3,32,2048]{2,1,0:T(8,128)(2,1)S(1)} collective-permute-done((bf16[3,32,2048]{2,1,0:T(8,128)(2,1)S(1)}, bf16[3,32,2048]{2,1,0:T(8,128)(2,1)S(1)}, u32[]{:S(2)}, u32[]{:S(2)}) %collective-permute-start.122) | collective-permute-done | bytes 393248 | tf_op jit(solution)/shard_map/ppermute | solution.py:50
  (1168 shorter events, 788.9 us)
Async XLA Ops:
  6.0 95.9 %collective-permute-start.19 = (bf16[256,512]{1,0:T(8,128)(2,1)}, bf16[256,512]{1,0:T(8,128)(2,1)}, u32[]{:S(2)}, u32[]{:S(2)}) collective-permute-start(bf16[256,512]{1,0:T(8,128)(2,1)} %dynamic-slice_bitcast_fusion.3), channel_id=1, source_target_pairs={{0,16},{16,0},{1,17},{17,1},{2,18},{18,2},{3,19},{19,3},{4,20},{20... | collective-permute-start | bytes 786440 | tf_op jit(solution)/shard_map/ppermute | solution.py:36
  25.0 129.4 %collective-permute-start.32 = (bf16[512,2,1024]{2,1,0:T(2,128)(2,1)}, bf16[512,2,1024]{2,1,0:T(2,128)(2,1)}, u32[]{:S(2)}, u32[]{:S(2)}) collective-permute-start(bf16[512,2,1024]{2,1,0:T(2,128)(2,1)} %dynamic-slice_bitcast_fusion), channel_id=1, source_target_pairs={{0,16},{16,0},{1,17},{17,1},{2,18},{18,2},{3,19},{19,3},{4,20},{20... | collective-permute-start | bytes 6291464 | tf_op jit(solution)/shard_map/ppermute | solution.py:36
  33.3 34.7 %collective-permute-start.3 = (bf16[3,32,2048]{2,1,0:T(8,128)(2,1)S(1)}, bf16[3,32,2048]{2,1,0:T(8,128)(2,1)S(1)}, u32[]{:S(2)}, u32[]{:S(2)}) collective-permute-start(bf16[3,32,2048]{2,1,0:T(8,128)(2,1)S(1)} %fusion.96), channel_id=1, source_target_pairs={{0,1},{1,2},{2,3},{3,0},{4,5},{5,6},{6,7},{7,4},{8,9},{9,10},{10,1... | collective-permute-start | bytes 1179656 | tf_op jit(solution)/shard_map/ppermute | solution.py:45
  42.9 44.0 %collective-permute-start.6 = (bf16[512,768]{0,1:T(8,128)(2,1)S(1)}, bf16[512,768]{0,1:T(8,128)(2,1)S(1)}, u32[]{:S(2)}, u32[]{:S(2)}) collective-permute-start(bf16[512,768]{0,1:T(8,128)(2,1)S(1)} %bitcast.487), channel_id=1, source_target_pairs={{0,4},{4,0},{8,12},{12,8},{1,5},{5,1},{9,13},{13,9},{2,6},{6,2},{1... | collective-permute-start | bytes 2359304 | tf_op jit(solution)/shard_map/ppermute | solution.py:58
  96.4 52.1 %collective-permute-start.37 = (bf16[1024,512]{1,0:T(8,128)(2,1)}, bf16[1024,512]{1,0:T(8,128)(2,1)}, u32[]{:S(2)}, u32[]{:S(2)}) collective-permute-start(bf16[1024,512]{1,0:T(8,128)(2,1)} %dynamic-slice_bitcast_fusion.1), channel_id=1, source_target_pairs={{0,16},{16,0},{1,17},{17,1},{2,18},{18,2},{3,19},{19,3},{4,20},{20... | collective-permute-start | bytes 3145736 | tf_op jit(solution)/shard_map/ppermute | solution.py:36
  160.9 63.7 %collective-permute-start.33 = (bf16[512,2048]{1,0:T(8,128)(2,1)S(1)}, bf16[512,2048]{1,0:T(8,128)(2,1)S(1)}, u32[]{:S(2)}, u32[]{:S(2)}) collective-permute-start(bf16[512,2048]{1,0:T(8,128)(2,1)S(1)} %bitcast.427), channel_id=1, source_target_pairs={{0,4},{4,0},{8,12},{12,8},{1,5},{5,1},{9,13},{13,9},{2,6},{6,2},{1... | collective-permute-start | bytes 6291464 | tf_op jit(solution)/shard_map/ppermute | solution.py:58
  162.3 62.9 %collective-permute-start.34 = (bf16[512,2048]{1,0:T(8,128)(2,1)S(1)}, bf16[512,2048]{1,0:T(8,128)(2,1)S(1)}, u32[]{:S(2)}, u32[]{:S(2)}) collective-permute-start(bf16[512,2048]{1,0:T(8,128)(2,1)S(1)} %bitcast.428), channel_id=1, source_target_pairs={{0,8},{4,12},{8,0},{12,4},{1,9},{5,13},{9,1},{13,5},{2,10},{6,14},... | collective-permute-start | bytes 6291464 | tf_op jit(solution)/shard_map/ppermute | solution.py:58
  183.0 94.4 %collective-permute-start.40 = (bf16[512,512]{1,0:T(8,128)(2,1)S(1)}, bf16[512,512]{1,0:T(8,128)(2,1)S(1)}, u32[]{:S(2)}, u32[]{:S(2)}) collective-permute-start(bf16[512,512]{1,0:T(8,128)(2,1)S(1)} %slice.1069), channel_id=1, source_target_pairs={{0,4},{4,0},{8,12},{12,8},{1,5},{5,1},{9,13},{13,9},{2,6},{6,2},{1... | collective-permute-start | bytes 1572872 | tf_op jit(solution)/shard_map/ppermute | solution.py:58
  225.2 52.2 %collective-permute-start.41 = (bf16[512,512]{1,0:T(8,128)(2,1)S(1)}, bf16[512,512]{1,0:T(8,128)(2,1)S(1)}, u32[]{:S(2)}, u32[]{:S(2)}) collective-permute-start(bf16[512,512]{1,0:T(8,128)(2,1)S(1)} %slice.1070), channel_id=1, source_target_pairs={{0,8},{4,12},{8,0},{12,4},{1,9},{5,13},{9,1},{13,5},{2,10},{6,14},... | collective-permute-start | bytes 1572872 | tf_op jit(solution)/shard_map/ppermute | solution.py:58
  290.1 38.4 %collective-permute-start.50 = (bf16[512,768]{0,1:T(8,128)(2,1)S(1)}, bf16[512,768]{0,1:T(8,128)(2,1)S(1)}, u32[]{:S(2)}, u32[]{:S(2)}) collective-permute-start(bf16[512,768]{0,1:T(8,128)(2,1)S(1)} %bitcast.483), channel_id=1, source_target_pairs={{0,4},{4,0},{8,12},{12,8},{1,5},{5,1},{9,13},{13,9},{2,6},{6,2},{1... | collective-permute-start | bytes 2359304 | tf_op jit(solution)/shard_map/ppermute | solution.py:58
  291.4 35.6 %collective-permute-start.51 = (bf16[512,768]{0,1:T(8,128)(2,1)S(1)}, bf16[512,768]{0,1:T(8,128)(2,1)S(1)}, u32[]{:S(2)}, u32[]{:S(2)}) collective-permute-start(bf16[512,768]{0,1:T(8,128)(2,1)S(1)} %bitcast.484), channel_id=1, source_target_pairs={{0,8},{4,12},{8,0},{12,4},{1,9},{5,13},{9,1},{13,5},{2,10},{6,14},... | collective-permute-start | bytes 2359304 | tf_op jit(solution)/shard_map/ppermute | solution.py:58
  324.1 36.2 %collective-permute-start.47 = (bf16[3,32,2048]{2,1,0:T(8,128)(2,1)S(1)}, bf16[3,32,2048]{2,1,0:T(8,128)(2,1)S(1)}, u32[]{:S(2)}, u32[]{:S(2)}) collective-permute-start(bf16[3,32,2048]{2,1,0:T(8,128)(2,1)S(1)} %get-tuple-element.167), channel_id=1, source_target_pairs={{0,2},{1,3},{2,0},{3,1},{4,6},{5,7},{6,4},{7,5},{8,10},{9,11},{10,... | collective-permute-start | bytes 1179656 | tf_op jit(solution)/shard_map/ppermute | solution.py:45
  412.5 74.8 %collective-permute-start.71 = (bf16[512,2048]{1,0:T(8,128)(2,1)S(1)}, bf16[512,2048]{1,0:T(8,128)(2,1)S(1)}, u32[]{:S(2)}, u32[]{:S(2)}) collective-permute-start(bf16[512,2048]{1,0:T(8,128)(2,1)S(1)} %bitcast.430), channel_id=1, source_target_pairs={{0,8},{4,12},{8,0},{12,4},{1,9},{5,13},{9,1},{13,5},{2,10},{6,14},... | collective-permute-start | bytes 6291464 | tf_op jit(solution)/shard_map/ppermute | solution.py:58
  414.2 74.0 %collective-permute-start.70 = (bf16[512,2048]{1,0:T(8,128)(2,1)S(1)}, bf16[512,2048]{1,0:T(8,128)(2,1)S(1)}, u32[]{:S(2)}, u32[]{:S(2)}) collective-permute-start(bf16[512,2048]{1,0:T(8,128)(2,1)S(1)} %bitcast.431), channel_id=1, source_target_pairs={{0,4},{4,0},{8,12},{12,8},{1,5},{5,1},{9,13},{13,9},{2,6},{6,2},{1... | collective-permute-start | bytes 6291464 | tf_op jit(solution)/shard_map/ppermute | solution.py:58
  414.9 66.9 %collective-permute-start.75 = (bf16[1024,512]{1,0:T(8,128)(2,1)S(1)}, bf16[1024,512]{1,0:T(8,128)(2,1)S(1)}, u32[]{:S(2)}, u32[]{:S(2)}) collective-permute-start(bf16[1024,512]{1,0:T(8,128)(2,1)S(1)} %copy-done.112), channel_id=1, source_target_pairs={{0,8},{4,12},{8,0},{12,4},{1,9},{5,13},{9,1},{13,5},{2,10},{6,14},... | collective-permute-start | bytes 3145736 | tf_op jit(solution)/shard_map/ppermute | solution.py:58
  416.6 66.5 %collective-permute-start.74 = (bf16[1024,512]{1,0:T(8,128)(2,1)S(1)}, bf16[1024,512]{1,0:T(8,128)(2,1)S(1)}, u32[]{:S(2)}, u32[]{:S(2)}) collective-permute-start(bf16[1024,512]{1,0:T(8,128)(2,1)S(1)} %copy-done.112), channel_id=1, source_target_pairs={{0,4},{4,0},{8,12},{12,8},{1,5},{5,1},{9,13},{13,9},{2,6},{6,2},{1... | collective-permute-start | bytes 3145736 | tf_op jit(solution)/shard_map/ppermute | solution.py:58
  417.5 72.8 %collective-permute-start.63 = (bf16[3,32,2048]{2,1,0:T(8,128)(2,1)S(1)}, bf16[3,32,2048]{2,1,0:T(8,128)(2,1)S(1)}, u32[]{:S(2)}, u32[]{:S(2)}) collective-permute-start(bf16[3,32,2048]{2,1,0:T(8,128)(2,1)S(1)} %get-tuple-element.294), channel_id=1, source_target_pairs={{0,1},{1,2},{2,3},{3,0},{4,5},{5,6},{6,7},{7,4},{8,9},{9,10},{10,1... | collective-permute-start | bytes 1179656 | tf_op jit(solution)/shard_map/ppermute | solution.py:50
  488.3 56.8 %collective-permute-start.73 = (bf16[256,2048]{1,0:T(8,128)(2,1)S(1)}, bf16[256,2048]{1,0:T(8,128)(2,1)S(1)}, u32[]{:S(2)}, u32[]{:S(2)}) collective-permute-start(bf16[256,2048]{1,0:T(8,128)(2,1)S(1)} %slice.1108), channel_id=1, source_target_pairs={{0,8},{4,12},{8,0},{12,4},{1,9},{5,13},{9,1},{13,5},{2,10},{6,14},... | collective-permute-start | bytes 3145736 | tf_op jit(solution)/shard_map/ppermute | solution.py:58
  512.5 47.7 %collective-permute-start.76 = (bf16[512,512]{1,0:T(8,128)(2,1)S(1)}, bf16[512,512]{1,0:T(8,128)(2,1)S(1)}, u32[]{:S(2)}, u32[]{:S(2)}) collective-permute-start(bf16[512,512]{1,0:T(8,128)(2,1)S(1)} %slice.1111), channel_id=1, source_target_pairs={{0,4},{4,0},{8,12},{12,8},{1,5},{5,1},{9,13},{13,9},{2,6},{6,2},{1... | collective-permute-start | bytes 1572872 | tf_op jit(solution)/shard_map/ppermute | solution.py:58
  520.8 39.4 %collective-permute-start.77 = (bf16[512,512]{1,0:T(8,128)(2,1)S(1)}, bf16[512,512]{1,0:T(8,128)(2,1)S(1)}, u32[]{:S(2)}, u32[]{:S(2)}) collective-permute-start(bf16[512,512]{1,0:T(8,128)(2,1)S(1)} %slice.1112), channel_id=1, source_target_pairs={{0,8},{4,12},{8,0},{12,4},{1,9},{5,13},{9,1},{13,5},{2,10},{6,14},... | collective-permute-start | bytes 1572872 | tf_op jit(solution)/shard_map/ppermute | solution.py:58
  720.2 52.3 %collective-permute-start.159 = (bf16[512,2048]{0,1:T(8,128)(2,1)S(1)}, bf16[512,2048]{0,1:T(8,128)(2,1)S(1)}, u32[]{:S(2)}, u32[]{:S(2)}) collective-permute-start(bf16[512,2048]{0,1:T(8,128)(2,1)S(1)} %pad_maximum_fusion.6), channel_id=1, source_target_pairs={{0,8},{4,12},{8,0},{12,4},{1,9},{5,13},{9,1},{13,5},{2,10},{6,14},... | collective-permute-start | bytes 6291464 | tf_op jit(solution)/shard_map/ppermute | solution.py:58
  720.9 53.0 %collective-permute-start.158 = (bf16[512,2048]{0,1:T(8,128)(2,1)S(1)}, bf16[512,2048]{0,1:T(8,128)(2,1)S(1)}, u32[]{:S(2)}, u32[]{:S(2)}) collective-permute-start(bf16[512,2048]{0,1:T(8,128)(2,1)S(1)} %pad_maximum_fusion.5), channel_id=1, source_target_pairs={{0,4},{4,0},{8,12},{12,8},{1,5},{5,1},{9,13},{13,9},{2,6},{6,2},{1... | collective-permute-start | bytes 6291464 | tf_op jit(solution)/shard_map/ppermute | solution.py:58
  761.0 36.9 %collective-permute-start.93 = (bf16[3,32,2048]{2,1,0:T(8,128)(2,1)S(1)}, bf16[3,32,2048]{2,1,0:T(8,128)(2,1)S(1)}, u32[]{:S(2)}, u32[]{:S(2)}) collective-permute-start(bf16[3,32,2048]{2,1,0:T(8,128)(2,1)S(1)} %get-tuple-element.50), channel_id=1, source_target_pairs={{0,2},{1,3},{2,0},{3,1},{4,6},{5,7},{6,4},{7,5},{8,10},{9,11},{10,... | collective-permute-start | bytes 1179656 | tf_op jit(solution)/shard_map/ppermute | solution.py:45
  964.2 153.7 %collective-permute-start.172 = (bf16[1024,512]{1,0:T(8,128)(2,1)}, bf16[1024,512]{1,0:T(8,128)(2,1)S(1)}, u32[]{:S(2)}, u32[]{:S(2)}) collective-permute-start(bf16[1024,512]{1,0:T(8,128)(2,1)} %pad_maximum_fusion.27), channel_id=1, source_target_pairs={{0,16},{1,17},{2,18},{3,19},{4,20},{5,21},{6,22},{7,23},{8,24},{9,... | collective-permute-start | bytes 3145736 | tf_op jit(solution)/shard_map/ppermute | solution.py:40
  1032.1 112.5 %collective-permute-start.155 = (bf16[512,2048]{0,1:T(8,128)(2,1)S(1)}, bf16[512,2048]{0,1:T(8,128)(2,1)S(1)}, u32[]{:S(2)}, u32[]{:S(2)}) collective-permute-start(bf16[512,2048]{0,1:T(8,128)(2,1)S(1)} %pad_maximum_fusion.3), channel_id=1, source_target_pairs={{0,8},{4,12},{8,0},{12,4},{1,9},{5,13},{9,1},{13,5},{2,10},{6,14},... | collective-permute-start | bytes 6291464 | tf_op jit(solution)/shard_map/ppermute | solution.py:58
  1054.3 102.9 %collective-permute-start.154 = (bf16[512,2048]{0,1:T(8,128)(2,1)S(1)}, bf16[512,2048]{0,1:T(8,128)(2,1)S(1)}, u32[]{:S(2)}, u32[]{:S(2)}) collective-permute-start(bf16[512,2048]{0,1:T(8,128)(2,1)S(1)} %pad_maximum_fusion.2), channel_id=1, source_target_pairs={{0,4},{4,0},{8,12},{12,8},{1,5},{5,1},{9,13},{13,9},{2,6},{6,2},{1... | collective-permute-start | bytes 6291464 | tf_op jit(solution)/shard_map/ppermute | solution.py:58
  1057.0 52.9 %collective-permute-start.166 = (bf16[512,512]{1,0:T(8,128)(2,1)S(1)}, bf16[512,512]{1,0:T(8,128)(2,1)S(1)}, u32[]{:S(2)}, u32[]{:S(2)}) collective-permute-start(bf16[512,512]{1,0:T(8,128)(2,1)S(1)} %get-tuple-element.220), channel_id=1, source_target_pairs={{0,8},{4,12},{8,0},{12,4},{1,9},{5,13},{9,1},{13,5},{2,10},{6,14},... | collective-permute-start | bytes 1572872 | tf_op jit(solution)/shard_map/ppermute | solution.py:58
  1058.4 56.8 %collective-permute-start.167 = (bf16[512,512]{1,0:T(8,128)(2,1)S(1)}, bf16[512,512]{1,0:T(8,128)(2,1)S(1)}, u32[]{:S(2)}, u32[]{:S(2)}) collective-permute-start(bf16[512,512]{1,0:T(8,128)(2,1)S(1)} %get-tuple-element.219), channel_id=1, source_target_pairs={{0,4},{4,0},{8,12},{12,8},{1,5},{5,1},{9,13},{13,9},{2,6},{6,2},{1... | collective-permute-start | bytes 1572872 | tf_op jit(solution)/shard_map/ppermute | solution.py:58
  1124.7 97.5 %collective-permute-start.162 = (bf16[512,2,1024]{2,1,0:T(2,128)(2,1)}, bf16[512,2,1024]{2,1,0:T(2,128)(2,1)}, u32[]{:S(2)}, u32[]{:S(2)}) collective-permute-start(bf16[512,2,1024]{2,1,0:T(2,128)(2,1)} %pad_maximum_fusion.7), channel_id=1, source_target_pairs={{0,16},{1,17},{2,18},{3,19},{4,20},{5,21},{6,22},{7,23},{8,24},{9,... | collective-permute-start | bytes 6291464 | tf_op jit(solution)/shard_map/ppermute | solution.py:40
  1139.3 179.2 %collective-permute-start.152 = (bf16[256,512]{1,0:T(8,128)(2,1)}, bf16[256,512]{1,0:T(8,128)(2,1)}, u32[]{:S(2)}, u32[]{:S(2)}) collective-permute-start(bf16[256,512]{1,0:T(8,128)(2,1)} %pad_maximum_fusion.52), channel_id=1, source_target_pairs={{0,16},{1,17},{2,18},{3,19},{4,20},{5,21},{6,22},{7,23},{8,24},{9,... | collective-permute-start | bytes 786440 | tf_op jit(solution)/shard_map/ppermute | solution.py:40
  1141.9 52.8 %collective-permute-start.173 = (bf16[1024,512]{1,0:T(8,128)(2,1)S(1)}, bf16[1024,512]{1,0:T(8,128)(2,1)S(1)}, u32[]{:S(2)}, u32[]{:S(2)}) collective-permute-start(bf16[1024,512]{1,0:T(8,128)(2,1)S(1)} %get-tuple-element.322), channel_id=1, source_target_pairs={{16,0},{17,1},{18,2},{19,3},{20,4},{21,5},{22,6},{23,7},{24,8},{25... | collective-permute-start | bytes 3145736 | tf_op jit(solution)/shard_map/ppermute | solution.py:40
  1336.1 45.7 %collective-permute-start.135 = (bf16[512,3,256]{0,2,1:T(8,128)(2,1)}, bf16[512,3,256]{0,2,1:T(8,128)(2,1)}, u32[]{:S(2)}, u32[]{:S(2)}) collective-permute-start(bf16[512,3,256]{0,2,1:T(8,128)(2,1)} %get-tuple-element.333), channel_id=1, source_target_pairs={{16,0},{17,1},{18,2},{19,3},{20,4},{21,5},{22,6},{23,7},{24,8},{25... | collective-permute-start | bytes 2359304 | tf_op jit(solution)/shard_map/ppermute | solution.py:40
  (350 other events, 4916.1 us)
where the time goes:
time: 1410 us; the launch traced here: 1390 us
  waiting for transfers between devices  693 us (49%)
  starting transfers between devices  261 us (19%)
  matrix products  158 us (11%)
  other arithmetic  139 us (10%)
  local copies, waits for them, and re-layouts  136 us (10%)
    ppermute x68, waiting for transfers between devices, across(): return lax.ppermute(block, 'dp', [(i, i ^ flip) for i in range(4)])  319 us
    ppermute x42, waiting for transfers between devices, from_ahead(): lax.ppermute(block, 'tensor', [(i, (i - distance) % size) for i in range(...  210 us
    ppermute x24, waiting for transfers between devices, to_ahead(): lax.ppermute(block, 'tensor', [(i, (i + distance) % size) for i in range(...  146 us
    ppermute x42, starting transfers between devices, from_ahead(): lax.ppermute(block, 'tensor', [(i, (i - distance) % size) for i in range(...  119 us
    ppermute x68, starting transfers between devices, across(): return lax.ppermute(block, 'dp', [(i, i ^ flip) for i in range(4)])  78.3 us
    dot_general x8, matrix products, inner_right(): lax.dot_general(left, right, (((1,), (1,)), ((), ())), preferred_element_...  63.1 us
    unnamed x487, local copies, waits for them, and re-layouts  60.4 us
    ppermute x24, starting transfers between devices, to_ahead(): lax.ppermute(block, 'tensor', [(i, (i + distance) % size) for i in range(...  39.8 us
  transfers between devices with their start and end apart: 174, of which 72 were waited for; matrix products, arithmetic and copies ran while one was open for 22% of the time, Pallas kernels for 0%

commit v1 on v0

--- a/solution.py
+++ b/solution.py
@@ -1,6 +1,8 @@
 import jax
 import jax.numpy as jnp
 from jax import lax
+from jax.experimental import pallas as pl
+from jax.experimental.pallas import tpu as pltpu
 from jax.sharding import PartitionSpec as P
 
 
@@ -10,6 +12,7 @@
 
 EPS = 1e-06
 THETA = 500000.0
+HIDDEN = -1e30
 
 
 def matmul(left, right):
@@ -133,16 +136,15 @@
     return total
 
 
-def sum_heads(parts, seqs):
+def head_parts(parts, seqs):
     size = lax.axis_size("tensor")
-    split = parts.reshape(parts.shape[0], seqs, 2, size, -1)
-    other = swap_cores(split)
-    chip = split + other[:, :, ::-1]
-    total = chip
+    other = swap_cores(parts)
+    turned_over = other.reshape(8, seqs, 2, -1)[:, :, ::-1].reshape(parts.shape)
+    chip = parts + turned_over
+    ahead = []
     for j in range(1, size):
-        ahead = from_ahead(chip, j)
-        total = total + jnp.roll(ahead, j, axis=3)
-    return total.reshape(parts.shape)
+        ahead.append(from_ahead(chip, j))
+    return [chip] + ahead
 
 
 def sum_gains(part):
@@ -177,34 +179,190 @@
     half_dim = HD // 2
     inverse_freq = THETA ** (-(jnp.arange(half_dim, dtype=jnp.float32) * (2.0 / HD)))
     angles = positions.astype(jnp.float32)[..., None] * inverse_freq
-    return (visible, jnp.cos(angles), jnp.sin(angles))
-
-
-def rotate(vectors, cosine, sine_part):
-    half_dim = HD // 2
-    front_half = vectors[..., :half_dim]
-    back_half = vectors[..., half_dim:]
-    cos_wide = cosine[:, :, None, :]
-    sin_wide = sine_part[:, :, None, :]
-    return jnp.concatenate(
-        [
-            front_half * cos_wide - back_half * sin_wide,
-            back_half * cos_wide + front_half * sin_wide,
-        ],
-        axis=-1,
-    )
-
-
-def masked_scores(query_rot, key_rot, visible):
-    scores = jnp.einsum(
-        "bshe,bthe->bhst", query_rot, key_rot, preferred_element_type=jnp.float32
-    ) * HD ** (-0.5)
-    return jnp.where(visible[:, None], scores, -jnp.inf)
-
-
-def log_norm(masked):
-    row_max = jnp.max(masked, axis=-1, keepdims=True)
-    return row_max + jnp.log(jnp.sum(jnp.exp(masked - row_max), axis=-1, keepdims=True))
+    cosine = jnp.cos(angles)
+    sine = jnp.sin(angles)
+    return (
+        jnp.where(visible, 0.0, HIDDEN),
+        jnp.concatenate([cosine, cosine], axis=-1),
+        jnp.concatenate([-sine, sine], axis=-1),
+    )
+
+
+def exact_dot(left, right, contract):
+    return lax.dot_general(
+        left,
+        right,
+        (contract, ((), ())),
+        precision=lax.Precision.HIGHEST,
+        preferred_element_type=jnp.float32,
+    )
+
+
+def token_sums(products):
+    shape = (8, products.shape[1])
+    row = lax.broadcasted_iota(jnp.int32, shape, 0)
+    col = lax.broadcasted_iota(jnp.int32, shape, 1)
+    low = (row == 0) & (col < shape[1] // 2)
+    high = (row == 1) & (col >= shape[1] // 2)
+    picks = jnp.where(low | high, 1.0, 0.0)
+    return exact_dot(picks, products, ((1,), (1,)))
+
+
+def column(values, row, width):
+    picks = lax.broadcasted_iota(jnp.int32, (8, width), 0) == row
+    return exact_dot(values, jnp.where(picks, 1.0, 0.0), ((0,), (0,)))
+
+
+def aligned_sum(refs):
+    tokens = refs[0].shape[1]
+    half = tokens // 2
+    turn = half // len(refs)
+    parts = []
+    for low in (0, half):
+        total = refs[0][:, low : low + half]
+        for j in range(1, len(refs)):
+            total = total + pltpu.roll(refs[j][:, low : low + half], turn * j, 1)
+        parts.append(total)
+    return jnp.concatenate(parts, axis=1)
+
+
+def turned(vectors, cosine, sine, sign):
+    return vectors * cosine + sign * (pltpu.roll(vectors, HD // 2, 1) * sine)
+
+
+def head_probs(query_rot, key_rot, bias):
+    scores = lax.dot_general(
+        query_rot, key_rot, (((1,), (1,)), ((), ())), preferred_element_type=jnp.float32
+    )
+    scores = scores * HD ** (-0.5) + bias
+    raised = jnp.exp(scores - jnp.max(scores, axis=1, keepdims=True))
+    return raised / jnp.sum(raised, axis=1, keepdims=True)
+
+
+def squares_kernel(qkv_ref, out_ref):
+    width = qkv_ref.shape[1] // 3
+    pair = qkv_ref[:, : 2 * width]
+    out_ref[...] = token_sums(pair * pair)
+
+
+def attend_kernel(*refs):
+    qkv_ref, gain_ref, bias_ref, cos_ref, sin_ref = refs[:5]
+    parts, (mix_ref, total_ref) = refs[5:-2], refs[-2:]
+    width = qkv_ref.shape[1] // 3
+    total = aligned_sum(parts)
+    total_ref[...] = total
+    scales = lax.rsqrt(total / D + EPS)
+    query_scale = column(scales, 0, HD)
+    key_scale = column(scales, 1, HD)
+    bias, cosine, sine = bias_ref[0], cos_ref[0], sin_ref[0]
+    for low in range(0, width, HD):
+        cols = slice(low, low + HD)
+        keys = slice(width + low, width + low + HD)
+        query_rot = turned(
+            qkv_ref[:, cols] * query_scale * gain_ref[0:1, cols], cosine, sine, 1.0
+        ).astype(jnp.bfloat16)
+        key_rot = turned(
+            qkv_ref[:, keys] * key_scale * gain_ref[1:2, cols], cosine, sine, 1.0
+        ).astype(jnp.bfloat16)
+        probs = head_probs(query_rot, key_rot, bias)
+        values = qkv_ref[:, 2 * width + low : 2 * width + low + HD].astype(jnp.bfloat16)
+        mix_ref[:, cols] = matmul(probs.astype(jnp.bfloat16), values).astype(jnp.bfloat16)
+
+
+def attend_back_kernel(
+    full_ref,
+    w_out_ref,
+    qkv_ref,
+    total_ref,
+    gain_ref,
+    bias_ref,
+    cos_ref,
+    sin_ref,
+    back_ref,
+    values_ref,
+    dots_ref,
+    gains_ref,
+    prod_ref,
+):
+    width = qkv_ref.shape[1] // 3
+
+    @pl.when(pl.program_id(0) == 0)
+    def _():
+        gains_ref[...] = jnp.zeros_like(gains_ref)
+
+    back_mix = inner_right(full_ref[...], w_out_ref[...]).astype(jnp.bfloat16)
+    scales = lax.rsqrt(total_ref[...] / D + EPS)
+    query_scale = column(scales, 0, HD)
+    key_scale = column(scales, 1, HD)
+    bias, cosine, sine = bias_ref[0], cos_ref[0], sin_ref[0]
+    for low in range(0, width, HD):
+        cols = slice(low, low + HD)
+        keys = slice(width + low, width + low + HD)
+        query_hat = qkv_ref[:, cols] * query_scale
+        key_hat = qkv_ref[:, keys] * key_scale
+        query_gain = gain_ref[0:1, cols]
+        key_gain = gain_ref[1:2, cols]
+        query_rot = turned(query_hat * query_gain, cosine, sine, 1.0).astype(jnp.bfloat16)
+        key_rot = turned(key_hat * key_gain, cosine, sine, 1.0).astype(jnp.bfloat16)
+        probs = head_probs(query_rot, key_rot, bias)
+        values = qkv_ref[:, 2 * width + low : 2 * width + low + HD].astype(jnp.bfloat16)
+        back = back_mix[:, cols]
+        values_ref[:, cols] = inner_left(probs.astype(jnp.bfloat16), back).astype(jnp.bfloat16)
+        back_probs = inner_right(back, values)
+        row_dot = jnp.sum(probs * back_probs, axis=1, keepdims=True)
+        back_scores = (probs * (back_probs - row_dot) * HD ** (-0.5)).astype(jnp.bfloat16)
+        back_query = turned(matmul(back_scores, key_rot), cosine, sine, -1.0)
+        back_key = turned(inner_left(back_scores, query_rot), cosine, sine, -1.0)
+        gains_ref[0:1, cols] += jnp.sum(back_query * query_hat, axis=0, keepdims=True)
+        gains_ref[1:2, cols] += jnp.sum(back_key * key_hat, axis=0, keepdims=True)
+        back_query = back_query * query_gain
+        back_key = back_key * key_gain
+        back_ref[:, cols] = back_query
+        back_ref[:, keys] = back_key
+        prod_ref[:, cols] = back_query * query_hat
+        prod_ref[:, keys] = back_key * key_hat
+    dots_ref[...] = token_sums(prod_ref[...])
+
+
+def settle_kernel(*refs):
+    qkv_ref, total_ref, back_ref, values_ref = refs[:4]
+    parts, out_ref = refs[4:-1], refs[-1]
+    width = qkv_ref.shape[1] // 3
+    means = aligned_sum(parts) / D
+    scales = lax.rsqrt(total_ref[...] / D + EPS)
+    for row, low in ((0, 0), (1, width)):
+        cols = slice(low, low + width)
+        scale = column(scales, row, width)
+        hat = qkv_ref[:, cols] * scale
+        out_ref[:, cols] = (scale * (back_ref[:, cols] - hat * column(means, row, width))).astype(
+            jnp.bfloat16
+        )
+    out_ref[:, 2 * width :] = values_ref[...]
+
+
+def by_sequence(kernel, seqs, operands, results, scratch=(), flops=0):
+    def spec(shape, which):
+        block = list(shape)
+        if which is None:
+            return pl.BlockSpec(shape, lambda s: (0,) * len(shape))
+        if which == "table":
+            block[0] = 1
+            return pl.BlockSpec(tuple(block), lambda s: (s,) + (0,) * (len(shape) - 1))
+        block[which] //= seqs
+        if which == 0:
+            return pl.BlockSpec(tuple(block), lambda s: (s, 0))
+        return pl.BlockSpec(tuple(block), lambda s: (0, s))
+
+    moved = sum(array.size * array.dtype.itemsize for array, _ in operands)
+    return pl.pallas_call(
+        kernel,
+        grid=(seqs,),
+        in_specs=[spec(array.shape, which) for array, which in operands],
+        out_specs=[spec(shape, which) for shape, _, which in results],
+        out_shape=[jax.ShapeDtypeStruct(shape, dtype) for shape, dtype, _ in results],
+        scratch_shapes=list(scratch),
+        cost_estimate=pl.CostEstimate(flops=flops, bytes_accessed=moved, transcendentals=0),
+    )(*[array for array, _ in operands])
 
 
 class Layer:
@@ -216,62 +374,45 @@
         self.gains = gains
         width = w_out.shape[0]
         whole = local_blocks(gains)
-        self.query_gain = lax.dynamic_slice_in_dim(whole[0], head_slot * width, width)
-        self.key_gain = lax.dynamic_slice_in_dim(whole[1], head_slot * width, width)
+        self.head_gains = lax.dynamic_slice_in_dim(whole, head_slot * width, width, 1).astype(
+            jnp.float32
+        )
         self.head_slot = head_slot
 
     def attend(self, layer_in, tables):
-        visible, cosine, sine_part = tables
         full = gather_tokens(layer_in.astype(jnp.bfloat16))
         seqs, slots, rows, _ = full.shape
         length = slots * rows
         tokens = seqs * length
         full = full.reshape(tokens, D)
         width = self.w_out.shape[0]
-        heads = width // HD
         qkv = matmul(full, self.w_qkv)
-        queries = qkv[:, :width]
-        key_vecs = qkv[:, width : 2 * width]
-        values = qkv[:, 2 * width :].astype(jnp.bfloat16).reshape(seqs, length, heads, HD)
-        squares = sum_heads(
-            jnp.stack([jnp.sum(queries * queries, axis=-1), jnp.sum(key_vecs * key_vecs, axis=-1)]),
+        bias, cosine, sine = tables
+        (squares,) = by_sequence(
+            squares_kernel,
             seqs,
-        )
-        scales = lax.rsqrt(squares / D + EPS)
-        query_scale = scales[0][:, None]
-        key_scale = scales[1][:, None]
-        query_hat = queries * query_scale
-        key_hat = key_vecs * key_scale
-        query_rot = rotate(
-            (query_hat * self.query_gain).reshape(seqs, length, heads, HD), cosine, sine_part
-        ).astype(jnp.bfloat16)
-        key_rot = rotate(
-            (key_hat * self.key_gain).reshape(seqs, length, heads, HD), cosine, sine_part
-        ).astype(jnp.bfloat16)
-        masked = masked_scores(query_rot, key_rot, visible)
-        log_total = log_norm(masked)
-        probs = jnp.exp(masked - log_total)
-        mix = jnp.einsum(
-            "bhst,bthe->bshe",
-            probs.astype(jnp.bfloat16),
-            values,
-            preferred_element_type=jnp.float32,
-        )
-        mix = mix.astype(jnp.bfloat16).reshape(tokens, width)
+            [(qkv, 0)],
+            [((8, tokens), jnp.float32, 1)],
+            flops=tokens * width * 64,
+        )
+        parts = head_parts(squares, seqs)
+        mix, total = by_sequence(
+            attend_kernel,
+            seqs,
+            [(qkv, 0), (self.head_gains, None)]
+            + [(table, "table") for table in (bias, cosine, sine)]
+            + [(part, 1) for part in parts],
+            [((tokens, width), jnp.bfloat16, 0), ((8, tokens), jnp.float32, 1)],
+            flops=tokens * length * width * 4,
+        )
         attn = scatter_tokens(matmul(mix, self.w_out).reshape(seqs, slots, rows, D))
         attn_scale = rms_scale(attn)
         attn_hat = attn * attn_scale
         hidden = layer_in + attn_hat * self.gains[2]
         kept = dict(
             full=full,
-            query_hat=query_hat,
-            key_hat=key_hat,
-            query_scale=query_scale,
-            key_scale=key_scale,
-            query_rot=query_rot,
-            key_rot=key_rot,
-            values=values,
-            log_total=log_total,
+            qkv=qkv,
+            total=total,
             mix=mix,
             attn_hat=attn_hat,
             attn_scale=attn_scale,
@@ -329,7 +470,6 @@
         return back_hidden, dict(down=grad_down, gate_up=grad_gate_up, gain_ffn=gain_ffn)
 
     def attend_back(self, back_hidden, kept):
-        visible, cosine, sine_part = kept["tables"]
         attn_hat = kept["attn_hat"]
         gain_attn = jnp.sum(back_hidden * attn_hat, axis=(0, 1))
         back_hat = back_hidden * self.gains[2]
@@ -343,65 +483,39 @@
         shape = full.shape
         full = full.reshape(-1, D)
         tokens = full.shape[0]
-        query_rot = kept["query_rot"]
-        key_rot = kept["key_rot"]
-        values = kept["values"]
-        heads_shape = values.shape
+        width = self.w_out.shape[0]
+        bias, cosine, sine = kept["tables"]
+        seqs, length = bias.shape[:2]
+        qkv, total = kept["qkv"], kept["total"]
+        back, back_values, dots, gain_heads = by_sequence(
+            attend_back_kernel,
+            seqs,
+            [(full, 0), (self.w_out, None), (qkv, 0), (total, 1), (self.head_gains, None)]
+            + [(table, "table") for table in (bias, cosine, sine)],
+            [
+                ((tokens, 2 * width), jnp.float32, 0),
+                ((tokens, width), jnp.bfloat16, 0),
+                ((8, tokens), jnp.float32, 1),
+                ((8, width), jnp.float32, None),
+            ],
+            scratch=[pltpu.VMEM((length, 2 * width), jnp.float32)],
+            flops=tokens * width * (2 * D + length * 10),
+        )
+        parts = head_parts(dots, seqs)
+        (back_qkv,) = by_sequence(
+            settle_kernel,
+            seqs,
+            [(qkv, 0), (total, 1), (back, 0), (back_values, 0)] + [(part, 1) for part in parts],
+            [((tokens, 3 * width), jnp.bfloat16, 0)],
+            flops=tokens * width * 64,
+        )
         grad_out = inner_left(kept["mix"], full)
-        back_mix = inner_right(full, self.w_out).astype(jnp.bfloat16).reshape(heads_shape)
-        masked = masked_scores(query_rot, key_rot, visible)
-        probs = jnp.exp(masked - kept["log_total"])
-        back_values = jnp.einsum(
-            "bhst,bshe->bthe",
-            probs.astype(jnp.bfloat16),
-            back_mix,
-            preferred_element_type=jnp.float32,
-        ).astype(jnp.bfloat16)
-        back_probs = jnp.einsum(
-            "bshe,bthe->bhst", back_mix, values, preferred_element_type=jnp.float32
-        )
-        row_dot = jnp.sum(probs * back_probs, axis=-1, keepdims=True)
-        back_scores = (probs * (back_probs - row_dot) * HD ** (-0.5)).astype(jnp.bfloat16)
-        back_query_rot = jnp.einsum(
-            "bhst,bthe->bshe", back_scores, key_rot, preferred_element_type=jnp.float32
-        )
-        back_key_rot = jnp.einsum(
-            "bhst,bshe->bthe", back_scores, query_rot, preferred_element_type=jnp.float32
-        )
-        width = self.w_out.shape[0]
-        back_query_gained = rotate(back_query_rot, cosine, -sine_part).reshape(tokens, width)
-        back_key_gained = rotate(back_key_rot, cosine, -sine_part).reshape(tokens, width)
-        query_hat = kept["query_hat"]
-        key_hat = kept["key_hat"]
-        gain_query = jnp.sum(back_query_gained * query_hat, axis=0)
-        gain_key = jnp.sum(back_key_gained * key_hat, axis=0)
-        back_query_hat = back_query_gained * self.query_gain
-        back_key_hat = back_key_gained * self.key_gain
-        dots = sum_heads(
-            jnp.stack(
-                [
-                    jnp.sum(back_query_hat * query_hat, axis=-1),
-                    jnp.sum(back_key_hat * key_hat, axis=-1),
-                ]
-            ),
-            shape[0],
-        )
-        back_query = kept["query_scale"] * (back_query_hat - query_hat * (dots[0] / D)[:, None])
-        back_key = kept["key_scale"] * (back_key_hat - key_hat * (dots[1] / D)[:, None])
-        back_qkv = jnp.concatenate(
-            [
-                back_query.astype(jnp.bfloat16),
-                back_key.astype(jnp.bfloat16),
-                back_values.reshape(tokens, width),
-            ],
-            axis=1,
-        )
         back_input = back_hidden + scatter_tokens(inner_right(back_qkv, self.w_qkv).reshape(shape))
         grad_qkv = inner_left(kept["full"], back_qkv)
         zero_width = jnp.zeros((2, D), jnp.float32)
         start = self.head_slot * width
         gain_heads = local_blocks(
-            lax.dynamic_update_slice(zero_width, jnp.stack([gain_query, gain_key]), (0, start))
+            lax.dynamic_update_slice(zero_width, gain_heads[:2], (0, start))
         )
         gain_part = jnp.concatenate([gain_heads, gain_attn[None]], axis=0)
         return back_input, dict(out=grad_out, qkv=grad_qkv, gains=gain_part)

time: 1410 us -> 1370 us (0.972)
  local copies, waits for them, and re-layouts: 136 us -> 73.2 us
  Pallas kernels: 0 us -> 57.6 us
  waiting for transfers between devices: 693 us -> 733 us
  matrix products: 158 us -> 124 us
  other arithmetic: 139 us -> 116 us
    pallas_call x0 -> x8, Pallas kernels: none -> 57.6 us  [by_sequence(): pl.pallas_call(kernel, grid=(seqs,), in_specs=[spec(array.shape, which) f...]
    unnamed x487 -> x307, local copies, waits for them, and re-layouts: 60.4 us -> 29.4 us
    ppermute x68, waiting for transfers between devices: 319 us -> 349 us  [across(): return lax.ppermute(block, 'dp', [(i, i ^ flip) for i in range(4)])]
    dot_general x12 -> x0, matrix products: 23.1 us -> none  [the longest x2 8.23 us: attend_back(): jnp.einsum('bhst,bthe->bshe', back_scores, key_rot, preferred_element_typ...]
    reshape x18 -> x0, local copies, waits for them, and re-layouts: 22.4 us -> none  [the longest x4 5.69 us: attend_back(): inner_right(full, self.w_out).astype(jnp.bfloat16).reshape(heads_shape)]
    dot_general x8 -> x6, matrix products: 63.1 us -> 51.1 us  [inner_right(): lax.dot_general(left, right, (((1,), (1,)), ((), ())), preferred_element_...]
  transfers between devices with their start and end apart: 174 -> 174, of which waited for: 72 -> 69; matrix products, arithmetic and copies ran while one was open for 22% -> 17% of each run, Pallas kernels for 0% -> 4%
where the time goes in v1:
time: 1370 us; the launch traced here: 1360 us
  waiting for transfers between devices  733 us (54%)
  starting transfers between devices  248 us (18%)
  matrix products  124 us (9%)
  other arithmetic  116 us (8%)
  local copies, waits for them, and re-layouts  73.2 us (5%)
  Pallas kernels  57.6 us (4%)
    ppermute x68, waiting for transfers between devices, across(): return lax.ppermute(block, 'dp', [(i, i ^ flip) for i in range(4)])  349 us
    ppermute x42, waiting for transfers between devices, from_ahead(): lax.ppermute(block, 'tensor', [(i, (i - distance) % size) for i in range(...  210 us
    ppermute x24, waiting for transfers between devices, to_ahead(): lax.ppermute(block, 'tensor', [(i, (i + distance) % size) for i in range(...  153 us
    ppermute x42, starting transfers between devices, from_ahead(): lax.ppermute(block, 'tensor', [(i, (i - distance) % size) for i in range(...  112 us
    ppermute x68, starting transfers between devices, across(): return lax.ppermute(block, 'dp', [(i, i ^ flip) for i in range(4)])  73.7 us
    pallas_call x8, Pallas kernels, by_sequence(): pl.pallas_call(kernel, grid=(seqs,), in_specs=[spec(array.shape, which) f...  57.6 us
    dot_general x6, matrix products, inner_right(): lax.dot_general(left, right, (((1,), (1,)), ((), ())), preferred_element_...  51.1 us
    ppermute x24, starting transfers between devices, to_ahead(): lax.ppermute(block, 'tensor', [(i, (i + distance) % size) for i in range(...  38 us
  transfers between devices with their start and end apart: 174, of which 69 were waited for; matrix products, arithmetic and copies ran while one was open for 17% of the time, Pallas kernels for 4%

profile of v1, /device:TPU:0, one launch (start us, length us, event | category | flops | bytes accessed | tf_op | source)
XLA Modules:
  0.0 1355.6 jit_solution(3418751515218572525)
XLA Ops:
  41.1 21.1 %collective-permute-done.2 = bf16[3,32,2048]{2,1,0:T(8,128)(2,1)S(1)} collective-permute-done((bf16[3,32,2048]{2,1,0:T(8,128)(2,1)S(1)}, bf16[3,32,2048]{2,1,0:T(8,128)(2,1)S(1)}, u32[]{:S(2)}, u32[]{:S(2)}) %collective-permute-start.2) | collective-permute-done | bytes 393248 | tf_op jit(solution)/shard_map/ppermute | solution.py:48
  64.6 17.4 %collective-permute-done.7 = bf16[512,768]{0,1:T(8,128)(2,1)S(1)} collective-permute-done((bf16[512,768]{0,1:T(8,128)(2,1)S(1)}, bf16[512,768]{0,1:T(8,128)(2,1)S(1)}, u32[]{:S(2)}, u32[]{:S(2)}) %collective-permute-start.7) | collective-permute-done | bytes 786464 | tf_op jit(solution)/shard_map/ppermute | solution.py:61
  153.7 13.9 %collective-permute-done.39 = bf16[1024,512]{1,0:T(8,128)(2,1)S(1)} collective-permute-done((bf16[1024,512]{1,0:T(8,128)(2,1)S(1)}, bf16[1024,512]{1,0:T(8,128)(2,1)S(1)}, u32[]{:S(2)}, u32[]{:S(2)}) %collective-permute-start.39) | collective-permute-done | bytes 1048608 | tf_op jit(solution)/shard_map/ppermute | solution.py:61
  172.0 14.8 %collective-permute-done.26 = bf16[3,32,2048]{2,1,0:T(8,128)(2,1)S(1)} collective-permute-done((bf16[3,32,2048]{2,1,0:T(8,128)(2,1)S(1)}, bf16[3,32,2048]{2,1,0:T(8,128)(2,1)S(1)}, u32[]{:S(2)}, u32[]{:S(2)}) %collective-permute-start.26) | collective-permute-done | bytes 393248 | tf_op jit(solution)/shard_map/ppermute | solution.py:53
  197.7 16.3 %collective-permute-done.33 = bf16[512,2048]{1,0:T(8,128)(2,1)S(1)} collective-permute-done((bf16[512,2048]{1,0:T(8,128)(2,1)S(1)}, bf16[512,2048]{1,0:T(8,128)(2,1)S(1)}, u32[]{:S(2)}, u32[]{:S(2)}) %collective-permute-start.33) | collective-permute-done | bytes 2097184 | tf_op jit(solution)/shard_map/ppermute | solution.py:61
  217.0 15.0 %collective-permute-done.29 = bf16[3,32,2048]{2,1,0:T(8,128)(2,1)S(1)} collective-permute-done((bf16[3,32,2048]{2,1,0:T(8,128)(2,1)S(1)}, bf16[3,32,2048]{2,1,0:T(8,128)(2,1)S(1)}, u32[]{:S(2)}, u32[]{:S(2)}) %collective-permute-start.29) | collective-permute-done | bytes 393248 | tf_op jit(solution)/shard_map/ppermute | solution.py:48
  233.9 13.1 collective-permute-done.35
  291.1 15.9 %collective-permute-done.44 = bf16[3,32,2048]{2,1,0:T(8,128)(2,1)S(1)} collective-permute-done((bf16[3,32,2048]{2,1,0:T(8,128)(2,1)S(1)}, bf16[3,32,2048]{2,1,0:T(8,128)(2,1)S(1)}, u32[]{:S(2)}, u32[]{:S(2)}) %collective-permute-start.44) | collective-permute-done | bytes 393248 | tf_op jit(solution)/shard_map/ppermute | solution.py:53
  326.0 25.0 %collective-permute-done.47 = bf16[3,32,2048]{2,1,0:T(8,128)(2,1)S(1)} collective-permute-done((bf16[3,32,2048]{2,1,0:T(8,128)(2,1)S(1)}, bf16[3,32,2048]{2,1,0:T(8,128)(2,1)S(1)}, u32[]{:S(2)}, u32[]{:S(2)}) %collective-permute-start.47) | collective-permute-done | bytes 393248 | tf_op jit(solution)/shard_map/ppermute | solution.py:48
  394.5 64.7 %collective-permute-done.75 = bf16[1024,512]{1,0:T(8,128)(2,1)S(1)} collective-permute-done((bf16[1024,512]{1,0:T(8,128)(2,1)S(1)}, bf16[1024,512]{1,0:T(8,128)(2,1)S(1)}, u32[]{:S(2)}, u32[]{:S(2)}) %collective-permute-start.75) | collective-permute-done | bytes 1048608 | tf_op jit(solution)/shard_map/ppermute | solution.py:61
  465.4 14.1 %collective-permute-done.64 = bf16[3,32,2048]{2,1,0:T(8,128)(2,1)S(1)} collective-permute-done((bf16[3,32,2048]{2,1,0:T(8,128)(2,1)S(1)}, bf16[3,32,2048]{2,1,0:T(8,128)(2,1)S(1)}, u32[]{:S(2)}, u32[]{:S(2)}) %collective-permute-start.64) | collective-permute-done | bytes 393248 | tf_op jit(solution)/shard_map/ppermute | solution.py:53
  500.0 24.2 %collective-permute-done.67 = bf16[3,32,2048]{2,1,0:T(8,128)(2,1)S(1)} collective-permute-done((bf16[3,32,2048]{2,1,0:T(8,128)(2,1)S(1)}, bf16[3,32,2048]{2,1,0:T(8,128)(2,1)S(1)}, u32[]{:S(2)}, u32[]{:S(2)}) %collective-permute-start.67) | collective-permute-done | bytes 393248 | tf_op jit(solution)/shard_map/ppermute | solution.py:48
  562.9 16.1 %collective-permute-done.80 = bf16[3,32,2048]{2,1,0:T(8,128)(2,1)S(1)} collective-permute-done((bf16[3,32,2048]{2,1,0:T(8,128)(2,1)S(1)}, bf16[3,32,2048]{2,1,0:T(8,128)(2,1)S(1)}, u32[]{:S(2)}, u32[]{:S(2)}) %collective-permute-start.80) | collective-permute-done | bytes 393248 | tf_op jit(solution)/shard_map/ppermute | solution.py:53
  599.7 24.2 %collective-permute-done.85 = bf16[3,32,2048]{2,1,0:T(8,128)(2,1)S(1)} collective-permute-done((bf16[3,32,2048]{2,1,0:T(8,128)(2,1)S(1)}, bf16[3,32,2048]{2,1,0:T(8,128)(2,1)S(1)}, u32[]{:S(2)}, u32[]{:S(2)}) %collective-permute-start.85) | collective-permute-done | bytes 393248 | tf_op jit(solution)/shard_map/ppermute | solution.py:48
  632.0 15.0 %multiply_convert_fusion.3 = (bf16[768,1024]{1,0:T(8,128)(2,1)}, bf16[768,1024]{1,0:T(8,128)(2,1)}) fusion(f32[768,2048]{1,0:T(8,128)S(1)} %fusion.102, bf16[768,2048]{1,0:T(8,128)(2,1)S(1)} %bitcast.396, bf16[512,512]{1,0:T(8,128)(2,1)S(1)} %copy-done.117, bf16[512,512]{1,0:T(8,128)(2,1)S(1)} %copy-done.115, bf16[1024,512]{1,0:T(8,128)(2,1)S(1)} %copy-done.76, ...), kind=kOutput, calls=%fused_computation.34 | convolution fusion | flops 3252420608 | bytes 16777216 | tf_op jit(solution)/shard_map/dot_general | solution.py:29
  674.4 13.5 collective-permute-done.169
  698.2 45.3 %collective-permute-done.170 = bf16[512,512]{1,0:T(8,128)(2,1)S(1)} collective-permute-done((bf16[512,512]{1,0:T(8,128)(2,1)S(1)}, bf16[512,512]{1,0:T(8,128)(2,1)S(1)}, u32[]{:S(2)}, u32[]{:S(2)}) %collective-permute-start.170) | collective-permute-done | bytes 524320 | tf_op jit(solution)/shard_map/ppermute | solution.py:61
  750.6 15.4 %collective-permute-done.90 = bf16[3,32,2048]{2,1,0:T(8,128)(2,1)S(1)} collective-permute-done((bf16[3,32,2048]{2,1,0:T(8,128)(2,1)S(1)}, bf16[3,32,2048]{2,1,0:T(8,128)(2,1)S(1)}, u32[]{:S(2)}, u32[]{:S(2)}) %collective-permute-start.90) | collective-permute-done | bytes 393248 | tf_op jit(solution)/shard_map/ppermute | solution.py:53
  785.9 25.9 %collective-permute-done.93 = bf16[3,32,2048]{2,1,0:T(8,128)(2,1)S(1)} collective-permute-done((bf16[3,32,2048]{2,1,0:T(8,128)(2,1)S(1)}, bf16[3,32,2048]{2,1,0:T(8,128)(2,1)S(1)}, u32[]{:S(2)}, u32[]{:S(2)}) %collective-permute-start.93) | collective-permute-done | bytes 393248 | tf_op jit(solution)/shard_map/ppermute | solution.py:48
  817.5 13.0 shard_map.130
  865.8 12.9 collective-permute-done.131
  905.7 14.1 %collective-permute-done.102 = bf16[3,32,2048]{2,1,0:T(8,128)(2,1)S(1)} collective-permute-done((bf16[3,32,2048]{2,1,0:T(8,128)(2,1)S(1)}, bf16[3,32,2048]{2,1,0:T(8,128)(2,1)S(1)}, u32[]{:S(2)}, u32[]{:S(2)}) %collective-permute-start.102) | collective-permute-done | bytes 393248 | tf_op jit(solution)/shard_map/ppermute | solution.py:53
  949.5 13.1 collective-permute-done.105
  1008.8 21.8 %collective-permute-done.165 = bf16[1024,512]{1,0:T(8,128)(2,1)} collective-permute-done((bf16[1024,512]{1,0:T(8,128)(2,1)S(1)}, bf16[1024,512]{1,0:T(8,128)(2,1)}, u32[]{:S(2)}, u32[]{:S(2)}) %collective-permute-start.165) | collective-permute-done | bytes 1048608 | tf_op jit(solution)/shard_map/ppermute | solution.py:61
  1035.9 50.3 %collective-permute-done.166 = bf16[512,512]{1,0:T(8,128)(2,1)} collective-permute-done((bf16[512,512]{1,0:T(8,128)(2,1)S(1)}, bf16[512,512]{1,0:T(8,128)(2,1)}, u32[]{:S(2)}, u32[]{:S(2)}) %collective-permute-start.166) | collective-permute-done | bytes 524320 | tf_op jit(solution)/shard_map/ppermute | solution.py:61
  1103.6 12.1 collective-permute-done.110
  1120.3 13.0 collective-permute-start.112
  1142.7 24.3 %collective-permute-done.113 = bf16[3,32,2048]{2,1,0:T(8,128)(2,1)S(1)} collective-permute-done((bf16[3,32,2048]{2,1,0:T(8,128)(2,1)S(1)}, bf16[3,32,2048]{2,1,0:T(8,128)(2,1)S(1)}, u32[]{:S(2)}, u32[]{:S(2)}) %collective-permute-start.113) | collective-permute-done | bytes 393248 | tf_op jit(solution)/shard_map/ppermute | solution.py:48
  1173.5 18.6 %collective-permute-done.156 = bf16[256,2048]{0,1:T(8,128)(2,1)S(1)} collective-permute-done((bf16[256,2048]{0,1:T(8,128)(2,1)S(1)}, bf16[256,2048]{0,1:T(8,128)(2,1)S(1)}, u32[]{:S(2)}, u32[]{:S(2)}) %collective-permute-start.156) | collective-permute-done | bytes 1048608 | tf_op jit(solution)/shard_map/ppermute | solution.py:61
  1212.7 13.0 shard_map.132
  1267.9 11.7 collective-permute-done.142
  1313.9 17.7 %collective-permute-done.122 = bf16[3,32,2048]{2,1,0:T(8,128)(2,1)S(1)} collective-permute-done((bf16[3,32,2048]{2,1,0:T(8,128)(2,1)S(1)}, bf16[3,32,2048]{2,1,0:T(8,128)(2,1)S(1)}, u32[]{:S(2)}, u32[]{:S(2)}) %collective-permute-start.122) | collective-permute-done | bytes 393248 | tf_op jit(solution)/shard_map/ppermute | solution.py:53
  (893 shorter events, 704.9 us)
Async XLA Ops:
  27.0 116.5 %collective-permute-start.32 = (bf16[512,2,1024]{2,1,0:T(2,128)(2,1)}, bf16[512,2,1024]{2,1,0:T(2,128)(2,1)}, u32[]{:S(2)}, u32[]{:S(2)}) collective-permute-start(bf16[512,2,1024]{2,1,0:T(2,128)(2,1)} %dynamic-slice_bitcast_fusion), channel_id=1, source_target_pairs={{0,16},{16,0},{1,17},{17,1},{2,18},{18,2},{3,19},{19,3},{4,20},{20... | collective-permute-start | bytes 6291464 | tf_op jit(solution)/shard_map/ppermute | solution.py:39
  27.9 110.9 %collective-permute-start.37 = (bf16[1024,512]{1,0:T(8,128)(2,1)}, bf16[1024,512]{1,0:T(8,128)(2,1)}, u32[]{:S(2)}, u32[]{:S(2)}) collective-permute-start(bf16[1024,512]{1,0:T(8,128)(2,1)} %dynamic-slice_bitcast_fusion.1), channel_id=1, source_target_pairs={{0,16},{16,0},{1,17},{17,1},{2,18},{18,2},{3,19},{19,3},{4,20},{20... | collective-permute-start | bytes 3145736 | tf_op jit(solution)/shard_map/ppermute | solution.py:39
  149.1 64.9 %collective-permute-start.33 = (bf16[512,2048]{1,0:T(8,128)(2,1)S(1)}, bf16[512,2048]{1,0:T(8,128)(2,1)S(1)}, u32[]{:S(2)}, u32[]{:S(2)}) collective-permute-start(bf16[512,2048]{1,0:T(8,128)(2,1)S(1)} %bitcast.355), channel_id=1, source_target_pairs={{0,4},{4,0},{8,12},{12,8},{1,5},{5,1},{9,13},{13,9},{2,6},{6,2},{1... | collective-permute-start | bytes 6291464 | tf_op jit(solution)/shard_map/ppermute | solution.py:61
  150.7 63.8 %collective-permute-start.34 = (bf16[512,2048]{1,0:T(8,128)(2,1)S(1)}, bf16[512,2048]{1,0:T(8,128)(2,1)S(1)}, u32[]{:S(2)}, u32[]{:S(2)}) collective-permute-start(bf16[512,2048]{1,0:T(8,128)(2,1)S(1)} %bitcast.356), channel_id=1, source_target_pairs={{0,8},{4,12},{8,0},{12,4},{1,9},{5,13},{9,1},{13,5},{2,10},{6,14},... | collective-permute-start | bytes 6291464 | tf_op jit(solution)/shard_map/ppermute | solution.py:61
  170.9 98.1 %collective-permute-start.40 = (bf16[512,512]{1,0:T(8,128)(2,1)S(1)}, bf16[512,512]{1,0:T(8,128)(2,1)S(1)}, u32[]{:S(2)}, u32[]{:S(2)}) collective-permute-start(bf16[512,512]{1,0:T(8,128)(2,1)S(1)} %slice.812), channel_id=1, source_target_pairs={{0,4},{4,0},{8,12},{12,8},{1,5},{5,1},{9,13},{13,9},{2,6},{6,2},{1... | collective-permute-start | bytes 1572872 | tf_op jit(solution)/shard_map/ppermute | solution.py:61
  214.6 54.5 %collective-permute-start.41 = (bf16[512,512]{1,0:T(8,128)(2,1)S(1)}, bf16[512,512]{1,0:T(8,128)(2,1)S(1)}, u32[]{:S(2)}, u32[]{:S(2)}) collective-permute-start(bf16[512,512]{1,0:T(8,128)(2,1)S(1)} %slice.813), channel_id=1, source_target_pairs={{0,8},{4,12},{8,0},{12,4},{1,9},{5,13},{9,1},{13,5},{2,10},{6,14},... | collective-permute-start | bytes 1572872 | tf_op jit(solution)/shard_map/ppermute | solution.py:61
  324.5 42.1 %collective-permute-start.59 = (bf16[256,512]{1,0:T(8,128)(2,1)S(1)}, bf16[256,512]{1,0:T(8,128)(2,1)S(1)}, u32[]{:S(2)}, u32[]{:S(2)}) collective-permute-start(bf16[256,512]{1,0:T(8,128)(2,1)S(1)} %copy-done.36), channel_id=1, source_target_pairs={{0,8},{4,12},{8,0},{12,4},{1,9},{5,13},{9,1},{13,5},{2,10},{6,14},... | collective-permute-start | bytes 786440 | tf_op jit(solution)/shard_map/ppermute | solution.py:61
  388.6 74.1 %collective-permute-start.71 = (bf16[512,2048]{1,0:T(8,128)(2,1)S(1)}, bf16[512,2048]{1,0:T(8,128)(2,1)S(1)}, u32[]{:S(2)}, u32[]{:S(2)}) collective-permute-start(bf16[512,2048]{1,0:T(8,128)(2,1)S(1)} %bitcast.358), channel_id=1, source_target_pairs={{0,8},{4,12},{8,0},{12,4},{1,9},{5,13},{9,1},{13,5},{2,10},{6,14},... | collective-permute-start | bytes 6291464 | tf_op jit(solution)/shard_map/ppermute | solution.py:61
  389.2 74.2 %collective-permute-start.70 = (bf16[512,2048]{1,0:T(8,128)(2,1)S(1)}, bf16[512,2048]{1,0:T(8,128)(2,1)S(1)}, u32[]{:S(2)}, u32[]{:S(2)}) collective-permute-start(bf16[512,2048]{1,0:T(8,128)(2,1)S(1)} %bitcast.359), channel_id=1, source_target_pairs={{0,4},{4,0},{8,12},{12,8},{1,5},{5,1},{9,13},{13,9},{2,6},{6,2},{1... | collective-permute-start | bytes 6291464 | tf_op jit(solution)/shard_map/ppermute | solution.py:61
  390.7 68.4 %collective-permute-start.75 = (bf16[1024,512]{1,0:T(8,128)(2,1)S(1)}, bf16[1024,512]{1,0:T(8,128)(2,1)S(1)}, u32[]{:S(2)}, u32[]{:S(2)}) collective-permute-start(bf16[1024,512]{1,0:T(8,128)(2,1)S(1)} %copy-done.55), channel_id=1, source_target_pairs={{0,8},{4,12},{8,0},{12,4},{1,9},{5,13},{9,1},{13,5},{2,10},{6,14},... | collective-permute-start | bytes 3145736 | tf_op jit(solution)/shard_map/ppermute | solution.py:61
  391.3 68.8 %collective-permute-start.74 = (bf16[1024,512]{1,0:T(8,128)(2,1)S(1)}, bf16[1024,512]{1,0:T(8,128)(2,1)S(1)}, u32[]{:S(2)}, u32[]{:S(2)}) collective-permute-start(bf16[1024,512]{1,0:T(8,128)(2,1)S(1)} %copy-done.55), channel_id=1, source_target_pairs={{0,4},{4,0},{8,12},{12,8},{1,5},{5,1},{9,13},{13,9},{2,6},{6,2},{1... | collective-permute-start | bytes 3145736 | tf_op jit(solution)/shard_map/ppermute | solution.py:61
  393.6 71.8 %collective-permute-start.63 = (bf16[3,32,2048]{2,1,0:T(8,128)(2,1)S(1)}, bf16[3,32,2048]{2,1,0:T(8,128)(2,1)S(1)}, u32[]{:S(2)}, u32[]{:S(2)}) collective-permute-start(bf16[3,32,2048]{2,1,0:T(8,128)(2,1)S(1)} %get-tuple-element.271), channel_id=1, source_target_pairs={{0,1},{1,2},{2,3},{3,0},{4,5},{5,6},{6,7},{7,4},{8,9},{9,10},{10,1... | collective-permute-start | bytes 1179656 | tf_op jit(solution)/shard_map/ppermute | solution.py:53
  463.5 61.0 %collective-permute-start.73 = (bf16[256,2048]{1,0:T(8,128)(2,1)S(1)}, bf16[256,2048]{1,0:T(8,128)(2,1)S(1)}, u32[]{:S(2)}, u32[]{:S(2)}) collective-permute-start(bf16[256,2048]{1,0:T(8,128)(2,1)S(1)} %slice.834), channel_id=1, source_target_pairs={{0,8},{4,12},{8,0},{12,4},{1,9},{5,13},{9,1},{13,5},{2,10},{6,14},... | collective-permute-start | bytes 3145736 | tf_op jit(solution)/shard_map/ppermute | solution.py:61
  491.2 48.5 %collective-permute-start.76 = (bf16[512,512]{1,0:T(8,128)(2,1)S(1)}, bf16[512,512]{1,0:T(8,128)(2,1)S(1)}, u32[]{:S(2)}, u32[]{:S(2)}) collective-permute-start(bf16[512,512]{1,0:T(8,128)(2,1)S(1)} %slice.837), channel_id=1, source_target_pairs={{0,4},{4,0},{8,12},{12,8},{1,5},{5,1},{9,13},{13,9},{2,6},{6,2},{1... | collective-permute-start | bytes 1572872 | tf_op jit(solution)/shard_map/ppermute | solution.py:61
  499.5 40.2 %collective-permute-start.77 = (bf16[512,512]{1,0:T(8,128)(2,1)S(1)}, bf16[512,512]{1,0:T(8,128)(2,1)S(1)}, u32[]{:S(2)}, u32[]{:S(2)}) collective-permute-start(bf16[512,512]{1,0:T(8,128)(2,1)S(1)} %slice.838), channel_id=1, source_target_pairs={{0,8},{4,12},{8,0},{12,4},{1,9},{5,13},{9,1},{13,5},{2,10},{6,14},... | collective-permute-start | bytes 1572872 | tf_op jit(solution)/shard_map/ppermute | solution.py:61
  673.9 103.6 %collective-permute-start.159 = (bf16[512,2048]{0,1:T(8,128)(2,1)S(1)}, bf16[512,2048]{0,1:T(8,128)(2,1)S(1)}, u32[]{:S(2)}, u32[]{:S(2)}) collective-permute-start(bf16[512,2048]{0,1:T(8,128)(2,1)S(1)} %pad_maximum_fusion.6), channel_id=1, source_target_pairs={{0,8},{4,12},{8,0},{12,4},{1,9},{5,13},{9,1},{13,5},{2,10},{6,14},... | collective-permute-start | bytes 6291464 | tf_op jit(solution)/shard_map/ppermute | solution.py:61
  690.2 53.2 %collective-permute-start.170 = (bf16[512,512]{1,0:T(8,128)(2,1)S(1)}, bf16[512,512]{1,0:T(8,128)(2,1)S(1)}, u32[]{:S(2)}, u32[]{:S(2)}) collective-permute-start(bf16[512,512]{1,0:T(8,128)(2,1)S(1)} %get-tuple-element.213), channel_id=1, source_target_pairs={{0,8},{4,12},{8,0},{12,4},{1,9},{5,13},{9,1},{13,5},{2,10},{6,14},... | collective-permute-start | bytes 1572872 | tf_op jit(solution)/shard_map/ppermute | solution.py:61
  691.8 53.0 %collective-permute-start.171 = (bf16[512,512]{1,0:T(8,128)(2,1)S(1)}, bf16[512,512]{1,0:T(8,128)(2,1)S(1)}, u32[]{:S(2)}, u32[]{:S(2)}) collective-permute-start(bf16[512,512]{1,0:T(8,128)(2,1)S(1)} %get-tuple-element.212), channel_id=1, source_target_pairs={{0,4},{4,0},{8,12},{12,8},{1,5},{5,1},{9,13},{13,9},{2,6},{6,2},{1... | collective-permute-start | bytes 1572872 | tf_op jit(solution)/shard_map/ppermute | solution.py:61
  695.0 52.1 %collective-permute-start.89 = (bf16[3,32,2048]{2,1,0:T(8,128)(2,1)S(1)}, bf16[3,32,2048]{2,1,0:T(8,128)(2,1)S(1)}, u32[]{:S(2)}, u32[]{:S(2)}) collective-permute-start(bf16[3,32,2048]{2,1,0:T(8,128)(2,1)S(1)} %get-tuple-element.261), channel_id=1, source_target_pairs={{0,1},{1,2},{2,3},{3,0},{4,5},{5,6},{6,7},{7,4},{8,9},{9,10},{10,1... | collective-permute-start | bytes 1179656 | tf_op jit(solution)/shard_map/ppermute | solution.py:53
  695.5 83.5 %collective-permute-start.158 = (bf16[512,2048]{0,1:T(8,128)(2,1)S(1)}, bf16[512,2048]{0,1:T(8,128)(2,1)S(1)}, u32[]{:S(2)}, u32[]{:S(2)}) collective-permute-start(bf16[512,2048]{0,1:T(8,128)(2,1)S(1)} %pad_maximum_fusion.5), channel_id=1, source_target_pairs={{0,4},{4,0},{8,12},{12,8},{1,5},{5,1},{9,13},{13,9},{2,6},{6,2},{1... | collective-permute-start | bytes 6291464 | tf_op jit(solution)/shard_map/ppermute | solution.py:61
  781.1 50.9 %collective-permute-start.160 = (bf16[256,2048]{0,1:T(8,128)(2,1)}, bf16[256,2048]{0,1:T(8,128)(2,1)}, u32[]{:S(2)}, u32[]{:S(2)}) collective-permute-start(bf16[256,2048]{0,1:T(8,128)(2,1)} %get-tuple-element.195), channel_id=1, source_target_pairs={{0,8},{4,12},{8,0},{12,4},{1,9},{5,13},{9,1},{13,5},{2,10},{6,14},... | collective-permute-start | bytes 3145736 | tf_op jit(solution)/shard_map/ppermute | solution.py:61
  785.3 46.7 %collective-permute-start.161 = (bf16[256,2048]{0,1:T(8,128)(2,1)}, bf16[256,2048]{0,1:T(8,128)(2,1)}, u32[]{:S(2)}, u32[]{:S(2)}) collective-permute-start(bf16[256,2048]{0,1:T(8,128)(2,1)} %get-tuple-element.194), channel_id=1, source_target_pairs={{0,4},{4,0},{8,12},{12,8},{1,5},{5,1},{9,13},{13,9},{2,6},{6,2},{1... | collective-permute-start | bytes 3145736 | tf_op jit(solution)/shard_map/ppermute | solution.py:61
  946.6 148.1 %collective-permute-start.172 = (bf16[1024,512]{1,0:T(8,128)(2,1)}, bf16[1024,512]{1,0:T(8,128)(2,1)}, u32[]{:S(2)}, u32[]{:S(2)}) collective-permute-start(bf16[1024,512]{1,0:T(8,128)(2,1)} %pad_maximum_fusion.25), channel_id=1, source_target_pairs={{0,16},{1,17},{2,18},{3,19},{4,20},{5,21},{6,22},{7,23},{8,24},{9,... | collective-permute-start | bytes 3145736 | tf_op jit(solution)/shard_map/ppermute | solution.py:43
  1008.0 112.4 %collective-permute-start.155 = (bf16[512,2048]{0,1:T(8,128)(2,1)S(1)}, bf16[512,2048]{0,1:T(8,128)(2,1)S(1)}, u32[]{:S(2)}, u32[]{:S(2)}) collective-permute-start(bf16[512,2048]{0,1:T(8,128)(2,1)S(1)} %pad_maximum_fusion.3), channel_id=1, source_target_pairs={{0,8},{4,12},{8,0},{12,4},{1,9},{5,13},{9,1},{13,5},{2,10},{6,14},... | collective-permute-start | bytes 6291464 | tf_op jit(solution)/shard_map/ppermute | solution.py:61
  1030.5 102.8 %collective-permute-start.154 = (bf16[512,2048]{0,1:T(8,128)(2,1)S(1)}, bf16[512,2048]{0,1:T(8,128)(2,1)S(1)}, u32[]{:S(2)}, u32[]{:S(2)}) collective-permute-start(bf16[512,2048]{0,1:T(8,128)(2,1)S(1)} %pad_maximum_fusion.2), channel_id=1, source_target_pairs={{0,4},{4,0},{8,12},{12,8},{1,5},{5,1},{9,13},{13,9},{2,6},{6,2},{1... | collective-permute-start | bytes 6291464 | tf_op jit(solution)/shard_map/ppermute | solution.py:61
  1033.1 53.2 %collective-permute-start.166 = (bf16[512,512]{1,0:T(8,128)(2,1)S(1)}, bf16[512,512]{1,0:T(8,128)(2,1)}, u32[]{:S(2)}, u32[]{:S(2)}) collective-permute-start(bf16[512,512]{1,0:T(8,128)(2,1)S(1)} %get-tuple-element.221), channel_id=1, source_target_pairs={{0,8},{4,12},{8,0},{12,4},{1,9},{5,13},{9,1},{13,5},{2,10},{6,14},... | collective-permute-start | bytes 1572872 | tf_op jit(solution)/shard_map/ppermute | solution.py:61
  1034.7 56.7 %collective-permute-start.167 = (bf16[512,512]{1,0:T(8,128)(2,1)S(1)}, bf16[512,512]{1,0:T(8,128)(2,1)}, u32[]{:S(2)}, u32[]{:S(2)}) collective-permute-start(bf16[512,512]{1,0:T(8,128)(2,1)S(1)} %get-tuple-element.220), channel_id=1, source_target_pairs={{0,4},{4,0},{8,12},{12,8},{1,5},{5,1},{9,13},{13,9},{2,6},{6,2},{1... | collective-permute-start | bytes 1572872 | tf_op jit(solution)/shard_map/ppermute | solution.py:61
  1101.0 101.1 %collective-permute-start.162 = (bf16[512,2,1024]{2,1,0:T(2,128)(2,1)}, bf16[512,2,1024]{2,1,0:T(2,128)(2,1)}, u32[]{:S(2)}, u32[]{:S(2)}) collective-permute-start(bf16[512,2,1024]{2,1,0:T(2,128)(2,1)} %pad_maximum_fusion.7), channel_id=1, source_target_pairs={{0,16},{1,17},{2,18},{3,19},{4,20},{5,21},{6,22},{7,23},{8,24},{9,... | collective-permute-start | bytes 6291464 | tf_op jit(solution)/shard_map/ppermute | solution.py:43
  1115.7 165.5 %collective-permute-start.152 = (bf16[256,512]{1,0:T(8,128)(2,1)}, bf16[256,512]{1,0:T(8,128)(2,1)}, u32[]{:S(2)}, u32[]{:S(2)}) collective-permute-start(bf16[256,512]{1,0:T(8,128)(2,1)} %pad_maximum_fusion.40), channel_id=1, source_target_pairs={{0,16},{1,17},{2,18},{3,19},{4,20},{5,21},{6,22},{7,23},{8,24},{9,... | collective-permute-start | bytes 786440 | tf_op jit(solution)/shard_map/ppermute | solution.py:43
  1118.3 52.2 %collective-permute-start.173 = (bf16[1024,512]{1,0:T(8,128)(2,1)S(1)}, bf16[1024,512]{1,0:T(8,128)(2,1)S(1)}, u32[]{:S(2)}, u32[]{:S(2)}) collective-permute-start(bf16[1024,512]{1,0:T(8,128)(2,1)S(1)} %get-tuple-element.299), channel_id=1, source_target_pairs={{16,0},{17,1},{18,2},{19,3},{20,4},{21,5},{22,6},{23,7},{24,8},{25... | collective-permute-start | bytes 3145736 | tf_op jit(solution)/shard_map/ppermute | solution.py:43
  1170.5 38.5 %collective-permute-start.115 = (bf16[3,4,32,2048]{3,2,0,1:T(8,128)(2,1)}, bf16[3,4,32,2048]{3,2,0,1:T(8,128)(2,1)}, u32[]{:S(2)}, u32[]{:S(2)}) collective-permute-start(bf16[3,4,32,2048]{3,2,0,1:T(8,128)(2,1)} %pad_maximum_fusion.19), channel_id=1, source_target_pairs={{0,16},{16,0},{1,17},{17,1},{2,18},{18,2},{3,19},{19,3},{4,20},{20... | collective-permute-start | bytes 4718600 | tf_op jit(solution)/shard_map/ppermute | solution.py:39
  1298.7 45.7 %collective-permute-start.135 = (bf16[512,3,256]{0,2,1:T(8,128)(2,1)}, bf16[512,3,256]{0,2,1:T(8,128)(2,1)}, u32[]{:S(2)}, u32[]{:S(2)}) collective-permute-start(bf16[512,3,256]{0,2,1:T(8,128)(2,1)} %get-tuple-element.302), channel_id=1, source_target_pairs={{16,0},{17,1},{18,2},{19,3},{20,4},{21,5},{22,6},{23,7},{24,8},{25... | collective-permute-start | bytes 2359304 | tf_op jit(solution)/shard_map/ppermute | solution.py:43
  (268 other events, 4958.0 us)
